TPU v7x, 256 devices: a whole 4x4x8 slice. The times are simulated.
256 devices in a mesh: expert: 64 (over z, y, core), dp: 4 (over x).
Axes of the slice: x: 4, y: 4, z: 8, core: 2. Of those that a mesh axis runs over, the one named last changes fastest.
Arguments:
- prenorm_input: bfloat16 [32768, 1280], P(('expert', 'dp')), may hold values from -6 to 6
- gain: float32 [1280], replicated, may hold values from 0.25 to 1.75
- router: bfloat16 [1280, 32], replicated, may hold values from -0.15625 to 0.15625
- routes: int32 [32768, 2], P(('expert', 'dp')), may hold values from 0 to 31, all different within a row; in each aligned block of 128 rows (0 to 127, 128 to 255, ...) at most 10 rows name the same one
- w_in: bfloat16 [64, 1280, 1280], P('expert', None, 'dp'), may hold values from -0.15625 to 0.15625
- w_out: bfloat16 [64, 1280, 1280], P('expert', 'dp'), may hold values from -0.125 to 0.125
- cotangent: bfloat16 [32768, 1280], P(('expert', 'dp')), may hold values from -18 to 18
Outputs:
- input_grad: bfloat16 [32768, 1280], P(('expert', 'dp'))
- grad_in: bfloat16 [64, 1280, 1280], P('expert', None, 'dp')
- grad_out: bfloat16 [64, 1280, 1280], P('expert', 'dp')
- grad_router: float32 [1280, 32], replicated
- grad_gain: float32 [1280], replicated
Inputs may be any that keep to these rules, and one draw needn't show every extreme that they name: `routes`: each row names 2 different experts; among the rows of one device no expert is named more than 10 times.
All inputs are finite; a program needn't handle non-finite values.
Results may differ from a plain program's by a relative error of at most 0.015.
Values may be sent and summed in bfloat16 or wider, within the bound.
A program may use at most 128 MiB of HBM per device.

v0:
```python
import math

import jax
import jax.numpy as jnp
from jax import lax
from jax.sharding import PartitionSpec as P


def gelu_parts(pre):
    coeff = math.sqrt(2.0 / math.pi)
    inner = coeff * (pre + 0.044715 * pre * pre * pre)
    tanh_val = jnp.tanh(inner)
    value = 0.5 * pre * (1.0 + tanh_val)
    slope = 0.5 * (1.0 + tanh_val) + 0.5 * pre * (1.0 - tanh_val * tanh_val) * coeff * (
        1.0 + 3.0 * 0.044715 * pre * pre
    )
    return (value, slope)


def norm_pieces(block, gain):
    values = block.astype(jnp.float32)
    centred_rows = values - jnp.mean(values, axis=1, keepdims=True)
    inverse_deviation = lax.rsqrt(
        jnp.mean(centred_rows * centred_rows, axis=1, keepdims=True) + 1e-06
    )
    normalized_rows = centred_rows * inverse_deviation
    return (
        normalized_rows,
        inverse_deviation,
        (normalized_rows * gain[None, :]).astype(jnp.bfloat16),
    )


def slot_index(routing_rows, expert_list, expert_capacity):
    flat = routing_rows.reshape(-1)
    onehot = (flat[:, None] == jnp.arange(expert_list, dtype=jnp.int32)[None, :]).astype(jnp.int32)
    before = jnp.cumsum(onehot, axis=0) - onehot
    slot = jnp.sum(before * onehot, axis=1)
    return flat * expert_capacity + slot


def expert_pass(rows_m, rows_d, column, w_first, w_second):
    gate = jax.nn.sigmoid(jnp.dot(rows_m, column, preferred_element_type=jnp.float32)[:, 0])
    pre = jnp.dot(rows_m, w_first, preferred_element_type=jnp.float32)
    value, slope = gelu_parts(pre)
    hidden = value.astype(jnp.bfloat16)
    back = jnp.dot(rows_d, w_second.T, preferred_element_type=jnp.float32)
    gate_gradient = jnp.sum(hidden.astype(jnp.float32) * back, axis=1)
    grad_pre = (gate[:, None] * back * slope).astype(jnp.bfloat16)
    grad_y = (gate[:, None] * rows_d.astype(jnp.float32)).astype(jnp.bfloat16)
    grad_second = jnp.dot(hidden.T, grad_y, preferred_element_type=jnp.float32)
    grad_first = jnp.dot(rows_m.T, grad_pre, preferred_element_type=jnp.float32)
    row_gradient = jnp.dot(grad_pre, w_first.T, preferred_element_type=jnp.float32)
    return (row_gradient, gate_gradient, grad_first, grad_second)


def body(prenorm_input, gain, router, routes, w_in, w_out, cotangent):
    halves = lax.axis_size("expert")
    expert_list = halves // 2
    groups = lax.axis_size("dp")
    tok_rows = prenorm_input.shape[0]
    top = routes.shape[1]
    width = prenorm_input.shape[1]
    expert_capacity = max(2, 5 * tok_rows * top // (4 * expert_list))
    slots = expert_list * expert_capacity
    hi = lax.Precision.HIGHEST
    normalized_rows, inverse_deviation, mixed_rows = norm_pieces(prenorm_input, gain)
    where = slot_index(routes, expert_list, expert_capacity)
    places = (where[None, :] == jnp.arange(slots, dtype=jnp.int32)[:, None]).astype(jnp.bfloat16)
    send_m = jnp.dot(
        places, jnp.repeat(mixed_rows, top, axis=0), preferred_element_type=jnp.float32
    ).astype(jnp.bfloat16)
    send_d = jnp.dot(
        places, jnp.repeat(cotangent, top, axis=0), preferred_element_type=jnp.float32
    ).astype(jnp.bfloat16)
    send_m = jnp.repeat(send_m.reshape(expert_list, expert_capacity, width), 2, axis=0)
    send_d = jnp.repeat(send_d.reshape(expert_list, expert_capacity, width), 2, axis=0)
    recv_m, recv_d = (
        lax.all_to_all(send_m, "expert", split_axis=0, concat_axis=0, tiled=True),
        lax.all_to_all(send_d, "expert", split_axis=0, concat_axis=0, tiled=True),
    )
    own = lax.axis_index("expert") // 2
    column = lax.dynamic_slice_in_dim(router, own, 1, 1)
    all_m, all_d = (
        lax.all_gather(recv_m[None], "dp", axis=0, tiled=True),
        lax.all_gather(recv_d[None], "dp", axis=0, tiled=True),
    )
    row_gradient, gate_gradient, grad_first, grad_second = expert_pass(
        all_m.reshape(-1, width), all_d.reshape(-1, width), column, w_in[0], w_out[0]
    )
    summed_rows, summed_gate = (
        lax.psum_scatter(
            row_gradient.reshape(groups, halves * expert_capacity, width).astype(jnp.bfloat16),
            "dp",
            scatter_dimension=0,
            tiled=True,
        ).astype(jnp.float32),
        lax.psum_scatter(
            gate_gradient.reshape(groups, halves * expert_capacity).astype(jnp.bfloat16),
            "dp",
            scatter_dimension=0,
            tiled=True,
        ).astype(jnp.float32),
    )
    back_rows = summed_rows[0].reshape(halves, expert_capacity, width)
    back_gate = summed_gate[0].reshape(halves, expert_capacity)
    grad_in = grad_first[None].astype(jnp.bfloat16)
    grad_out = grad_second[None].astype(jnp.bfloat16)
    ret_rows, ret_gate = (
        lax.all_to_all(
            back_rows.astype(jnp.bfloat16), "expert", split_axis=0, concat_axis=0, tiled=True
        ).astype(back_rows.dtype),
        lax.all_to_all(
            back_gate.astype(jnp.bfloat16), "expert", split_axis=0, concat_axis=0, tiled=True
        ).astype(back_gate.dtype),
    )
    pair_rows = jnp.sum(ret_rows.reshape(expert_list, 2, expert_capacity, width), axis=1).reshape(
        slots, width
    )
    pair_gate = jnp.sum(ret_gate.reshape(expert_list, 2, expert_capacity), axis=1).reshape(slots)
    grad_expert = jnp.sum(jnp.take(pair_rows, where, axis=0).reshape(tok_rows, top, width), axis=1)
    dgate_tok = jnp.take(pair_gate, where, axis=0).reshape(tok_rows, top)
    logits = jnp.dot(mixed_rows, router, preferred_element_type=jnp.float32)
    choose = (routes[:, :, None] == jnp.arange(expert_list, dtype=jnp.int32)[None, None, :]).astype(
        jnp.float32
    )
    gates = jax.nn.sigmoid(jnp.sum(choose * logits[:, None, :], axis=2))
    dlogit = jnp.sum(choose * (dgate_tok * gates * (1.0 - gates))[:, :, None], axis=1)
    mixed_gradient = grad_expert + jnp.dot(dlogit, router.astype(jnp.float32).T, precision=hi)
    router_term = jnp.dot(mixed_rows.astype(jnp.float32).T, dlogit, precision=hi)
    gain_product = jnp.sum(mixed_gradient * normalized_rows, axis=0)
    grad_router, grad_gain = lax.psum((router_term, gain_product), ("expert", "dp"))
    scaled_rows = mixed_gradient * gain[None, :]
    mean_first_term = jnp.mean(scaled_rows, axis=1, keepdims=True)
    mean_second_term = jnp.mean(scaled_rows * normalized_rows, axis=1, keepdims=True)
    norm_backward = inverse_deviation * (
        scaled_rows - mean_first_term - normalized_rows * mean_second_term
    )
    input_grad = (cotangent.astype(jnp.float32) + norm_backward).astype(jnp.bfloat16)
    return (input_grad, grad_in, grad_out, grad_router, grad_gain)


def solution(mesh):
    in_specs = (
        P(("expert", "dp"), None),
        P(),
        P(),
        P(("expert", "dp"), None),
        P("expert", None, "dp"),
        P("expert", "dp", None),
        P(("expert", "dp"), None),
    )
    out_specs = (
        P(("expert", "dp"), None),
        P("expert", None, "dp"),
        P("expert", "dp", None),
        P(),
        P(),
    )
    return jax.shard_map(body, mesh=mesh, in_specs=in_specs, out_specs=out_specs, check_vma=False)
```

profile of v0, /device:TPU:1, one launch (start us, length us, event | category | flops | bytes accessed | tf_op | source)
XLA Modules:
  0.0 642.1 jit_solution(16606466589608056609)
XLA Ops:
  15.1 75.7 %all_to_all.21 = bf16[64,10,1280]{2,1,0:T(8,128)(2,1)S(1)} all-to-all(bf16[64,10,1280]{2,1,0:T(8,128)(2,1)S(1)} %bitcast.60), channel_id=1, replica_groups=mesh['expert'=64,'dp'=4] {'expert'}, dimensions={0} | all-to-all | bytes 3276800 | tf_op jit(solution)/shard_map/all_to_all | solution.py:79
  90.8 1.7 copy.53
  94.1 68.1 %all_to_all.22 = bf16[64,10,1280]{2,1,0:T(8,128)(2,1)S(1)} all-to-all(bf16[64,10,1280]{2,1,0:T(8,128)(2,1)S(1)} %bitcast.61), channel_id=1, replica_groups=mesh['expert'=64,'dp'=4] {'expert'}, dimensions={0} | all-to-all | bytes 3276800 | tf_op jit(solution)/shard_map/all_to_all | solution.py:80
  162.2 1.6 copy.55
  163.9 11.2 %copy.54 = bf16[256,10,1280]{2,1,0:T(8,128)(2,1)} copy(bf16[256,10,1280]{2,0,1:T(8,128)(2,1)} %all-gather.5.cloned.1.call-done) | data formatting | bytes 13107200 | tf_op jit(solution)/shard_map/all_gather | solution.py:85
  175.2 13.0 %reshape.183 = bf16[2560,1280]{1,0:T(8,128)(2,1)} reshape(bf16[256,10,1280]{2,1,0:T(8,128)(2,1)} %copy.54) | data formatting | bytes 13107200 | tf_op jit(solution)/shard_map/reshape | solution.py:89
  188.2 4.9 convolution_reduce_fusion
  193.2 4.1 fusion.15
  197.2 34.7 %all-gather.7.cloned.1.call-done = bf16[256,10,1280]{2,0,1:T(8,128)(2,1)} async-done(((bf16[64,10,1280]{2,0,1:T(8,128)(2,1)}), bf16[256,10,1280]{2,0,1:T(8,128)(2,1)}) %all-gather.7.cloned.1.call-update) | async-done | bytes 6553616 | tf_op jit(solution)/shard_map/all_gather | solution.py:86
  231.9 10.8 %copy.56 = bf16[256,10,1280]{2,1,0:T(8,128)(2,1)} copy(bf16[256,10,1280]{2,0,1:T(8,128)(2,1)} %all-gather.7.cloned.1.call-done) | data formatting | bytes 13107200 | tf_op jit(solution)/shard_map/all_gather | solution.py:86
  242.8 12.8 %reshape.188 = bf16[2560,1280]{1,0:T(8,128)(2,1)} reshape(bf16[256,10,1280]{2,1,0:T(8,128)(2,1)} %copy.56) | data formatting | bytes 13107200 | tf_op jit(solution)/shard_map/reshape | solution.py:89
  255.6 8.9 %multiply_reduce_fusion = (bf16[2560]{0:T(1024)(128)(2,1)S(1)}, bf16[2560,320]{0,1:T(8,128)(2,1)S(1)}) fusion(f32[2560,320]{0,1:T(8,128)} %fusion.15, f32[2560]{0:T(1024)S(1)} %add_divide_fusion, bf16[2560,1280]{1,0:T(8,128)(2,1)} %reshape.188, bf16[1,320,1280]{2,1,0:T(8,128)(2,1)S(1)} %copy-done.14), kind=kOutput, calls=%fused_computation.16 | convolution fusion | flops 2117629440 | bytes 12303360 | tf_op jit(solution)/shard_map/dot_general | solution.py:47
  264.6 5.6 convolution_convert_fusion
  271.4 7.0 %all-reduce = bf16[4,640]{1,0:T(4,128)(2,1)S(1)} all-reduce(bf16[4,640]{1,0:T(4,128)(2,1)S(1)} %convert_element_type.107), channel_id=5, replica_groups=mesh['expert'=64,'dp'=4] {'dp'}, use_global_device_ids=true, to_apply=%region_9.10.clone | all-reduce | flops 2560 | bytes 10240
  279.9 13.2 %all-to-all-start.3 = ((bf16[64,1,10]{2,1,0:T(2,128)(2,1)}), bf16[64,1,10]{2,1,0:T(2,128)(2,1)S(1)}, u32[]{:S(2)}, u32[]{:S(2)}) async-start(bf16[64,1,10]{2,1,0:T(2,128)(2,1)} %convert_element_type.119), calls=%async_computation.4 | async-start | bytes 65536 | tf_op jit(solution)/shard_map/all_to_all | solution.py:113
  293.1 46.7 %reduce-scatter.2.cloned.1.call-done = bf16[1,640,1280]{2,1,0:T(8,128)(2,1)} async-done(((bf16[4,640,1280]{2,1,0:T(8,128)(2,1)}), bf16[1,640,1280]{2,1,0:T(8,128)(2,1)}) %reduce-scatter.2.cloned.1.call-update) | async-done | bytes 1638416 | tf_op jit(solution)/shard_map/reduce_scatter | solution.py:92
  339.8 4.0 convert_element_type.103
  344.4 10.7 %all-to-all-start.2 = ((bf16[64,10,1280]{2,1,0:T(8,128)(2,1)}), bf16[64,10,1280]{2,1,0:T(8,128)(2,1)S(1)}, u32[]{:S(2)}, u32[]{:S(2)}) async-start(bf16[64,10,1280]{2,1,0:T(8,128)(2,1)} %convert_element_type.103), calls=%async_computation.3 | async-start | bytes 5242880 | tf_op jit(solution)/shard_map/all_to_all | solution.py:110
  357.7 1.4 copy.51
  360.9 6.7 %fusion.10 = bf16[1,1280,320]{1,2,0:T(8,128)(2,1)} fusion(bf16[2560,320]{0,1:T(8,128)(2,1)} %copy-done.15, bf16[2560,1280]{1,0:T(8,128)(2,1)} %reshape.183), kind=kOutput, calls=%fused_computation.22 | convolution fusion | flops 2097561600 | bytes 9011200 | tf_op jit(solution)/shard_map/dot_general | solution.py:52
  367.6 6.9 %fusion.11 = bf16[1,320,1280]{2,1,0:T(8,128)(2,1)} fusion(bf16[2560,1280]{1,0:T(8,128)(2,1)} %reshape.188, f32[2560]{0:T(1024)S(1)} %add_divide_fusion, f32[2560,320]{0,1:T(8,128)S(1)} %copy-done.17), kind=kOutput, calls=%fused_computation.23 | convolution fusion | flops 2114764800 | bytes 10659840 | tf_op jit(solution)/shard_map/dot_general | solution.py:51
  376.1 2.2 gather_fusion.1
  382.7 1.9 fusion.42
  384.6 31.6 %all-to-all-done.2 = bf16[64,10,1280]{2,1,0:T(8,128)(2,1)S(1)} async-done(((bf16[64,10,1280]{2,1,0:T(8,128)(2,1)}), bf16[64,10,1280]{2,1,0:T(8,128)(2,1)S(1)}, u32[]{:S(2)}, u32[]{:S(2)}) %all-to-all-start.2) | async-done | bytes 1638432 | tf_op jit(solution)/shard_map/all_to_all | solution.py:110
  416.2 2.0 convert_reduce_fusion
  418.2 1.9 reshape.191
  420.1 2.2 gather_fusion
  422.3 2.1 gather.13
  424.5 1.7 select_reduce_fusion
  428.0 75.6 %psum.15 = f32[1280]{0:T(1024)} all-reduce(f32[1280]{0:T(1024)S(1)} %get-tuple-element.5), channel_id=1, replica_groups=mesh['expert'=64,'dp'=4] {'expert','dp'}, use_global_device_ids=true, to_apply=%region_17.18 | all-reduce | flops 1280 | bytes 10240 | tf_op jit(solution)/shard_map/psum | solution.py:132
  503.6 130.3 %all-reduce.3.cloned.1.call-done = f32[1280,32]{0,1:T(8,128)} async-done(((f32[1280,32]{0,1:T(8,128)}), f32[1280,32]{0,1:T(8,128)}) %all-reduce.3.cloned.1.call-update) | async-done | bytes 163856 | tf_op jit(solution)/shard_map/psum | solution.py:132
  634.0 1.6 copy.69
  (95 shorter events, 24.9 us)
Async XLA Ops:
  7.2 186.0 %copy-start = (bf16[1,1280,320]{1,2,0:T(8,128)(2,1)S(1)}, bf16[1,1280,320]{1,2,0:T(8,128)(2,1)}, u32[]{:S(2)}) copy-start(bf16[1,1280,320]{1,2,0:T(8,128)(2,1)} %param.11) | copy-start | bytes 2457604
  7.2 156.7 %all-gather.5.cloned.1.call-start = ((), (), s32[]{:S(2)}) async-start(), calls=%async_computation.7 | async-start | bytes 8192000 | tf_op jit(solution)/shard_map/all_gather | solution.py:85
  11.6 3.3 copy-start.12
  12.9 0.7 copy-start.3
  90.8 1.7 copy-start.4
  92.5 139.5 %all-gather.7.cloned.1.call-start = ((), (), s32[]{:S(2)}) async-start(), calls=%async_computation.8 | async-start | bytes 8192000 | tf_op jit(solution)/shard_map/all_gather | solution.py:86
  163.8 176.0 %reduce-scatter.2.cloned.1.call-start = ((), (), s32[]{:S(2)}) async-start(), calls=%async_computation.5 | async-start | bytes 8192000 | tf_op jit(solution)/shard_map/reduce_scatter | solution.py:92
  175.2 13.0 %copy-start.6 = (bf16[1280,32]{0,1:T(8,128)(2,1)S(1)}, bf16[1280,32]{0,1:T(8,128)(2,1)}, u32[]{:S(2)}) copy-start(bf16[1280,32]{0,1:T(8,128)(2,1)} %param.9) | copy-start | bytes 245764
  188.2 5.0 copy-start.1
  242.8 12.8 %copy-start.14 = (bf16[1,320,1280]{2,1,0:T(8,128)(2,1)S(1)}, bf16[1,320,1280]{2,1,0:T(8,128)(2,1)}, u32[]{:S(2)}) copy-start(bf16[1,320,1280]{2,1,0:T(8,128)(2,1)} %param.12) | copy-start | bytes 2457604
  264.6 5.6 copy-start.15
  270.1 0.7 copy-start.16
  279.9 63.9 %all-to-all-start.3 = ((bf16[64,1,10]{2,1,0:T(2,128)(2,1)}), bf16[64,1,10]{2,1,0:T(2,128)(2,1)S(1)}, u32[]{:S(2)}, u32[]{:S(2)}) async-start(bf16[64,1,10]{2,1,0:T(2,128)(2,1)} %convert_element_type.119), calls=%async_computation.4 | async-start | bytes 65536 | tf_op jit(solution)/shard_map/all_to_all | solution.py:113
  343.8 12.2 %copy-start.11 = (s32[128,2]{0,1:T(2,128)S(1)}, s32[128,2]{0,1:T(2,128)}, u32[]{:S(2)}) copy-start(s32[128,2]{0,1:T(2,128)} %param.10) | copy-start | bytes 3076
  343.8 0.6 copy-start.7
  344.4 71.8 %all-to-all-start.2 = ((bf16[64,10,1280]{2,1,0:T(8,128)(2,1)}), bf16[64,10,1280]{2,1,0:T(8,128)(2,1)S(1)}, u32[]{:S(2)}, u32[]{:S(2)}) async-start(bf16[64,10,1280]{2,1,0:T(8,128)(2,1)} %convert_element_type.103), calls=%async_computation.3 | async-start | bytes 5242880 | tf_op jit(solution)/shard_map/all_to_all | solution.py:110
  355.1 278.8 %all-reduce.3.cloned.1.call-start = ((), (), s32[]{:S(2)}) async-start(), calls=%async_computation.6 | async-start | bytes 327680 | tf_op jit(solution)/shard_map/psum | solution.py:132
  360.9 6.7 %copy-start.17 = (f32[2560,320]{0,1:T(8,128)S(1)}, f32[2560,320]{0,1:T(8,128)}, u32[]{:S(2)}) copy-start(f32[2560,320]{0,1:T(8,128)} %fusion.15) | copy-start | bytes 9830404
  367.6 6.9 %copy-start.8 = (bf16[64,1,10]{2,1,0:T(2,128)(2,1)S(1)}, bf16[64,1,10]{2,1,0:T(2,128)(2,1)}, u32[]{:S(2)}) copy-start(bf16[64,1,10]{2,1,0:T(2,128)(2,1)} %copy-done.7) | copy-start | bytes 3844
  420.1 4.4 copy-start.10
  422.3 3.9 copy-start.2
  422.3 3.9 copy-start.9
  422.3 3.9 copy-start.13
  422.3 4.6 copy-start.5
Sparse Core Ops, SparseCore 0:
  92.6 66.4 all-gather.4
  164.0 67.9 all-gather.6
  270.3 69.4 reduce-scatter.1
  384.7 249.2 all-reduce.2
where the time goes:
time: 644 us; the launch traced here: 642 us
  waiting for transfers between devices  243 us (38%)
  blocking collectives  226 us (35%)
  local copies, waits for them, and re-layouts  79.3 us (12%)
  matrix products  41.6 us (6%)
  starting transfers between devices  24.1 us (4%)
  between operations  14.1 us (2%)
  other arithmetic  13.1 us (2%)
    psum x1, waiting for transfers between devices, body(): lax.psum((router_term, gain_product), ('expert', 'dp'))  130 us
    all_to_all x1, blocking collectives, body(): lax.all_to_all(send_m, 'expert', split_axis=0, concat_axis=0, tiled=True)  75.7 us
    psum x1, blocking collectives, body(): lax.psum((router_term, gain_product), ('expert', 'dp'))  75.6 us
    all_to_all x1, blocking collectives, body(): lax.all_to_all(send_d, 'expert', split_axis=0, concat_axis=0, tiled=True)  68.1 us
    reduce_scatter x1, waiting for transfers between devices, body(): lax.psum_scatter(row_gradient.reshape(groups, halves * expert_capacity, w...  46.7 us
    all_gather x1, waiting for transfers between devices, body(): lax.all_gather(recv_d[None], 'dp', axis=0, tiled=True)  34.7 us
    all_to_all x1, waiting for transfers between devices, body(): lax.all_to_all(back_rows.astype(jnp.bfloat16), 'expert', split_axis=0, co...  31.6 us
    all_to_all x1, starting transfers between devices, body(): lax.all_to_all(back_gate.astype(jnp.bfloat16), 'expert', split_axis=0, co...  13.2 us
  transfers between devices with their start and end apart: 6, of which 4 were waited for; matrix products, arithmetic and copies ran while one was open for 13% of the time, Pallas kernels for 0%

commit v1 on v0

v1 whole, which is shorter than its diff:
```python
import math

import jax
import jax.numpy as jnp
from jax import lax
from jax.sharding import PartitionSpec as P

F32 = jnp.float32
BF16 = jnp.bfloat16


def gelu_parts(pre):
    coeff = math.sqrt(2.0 / math.pi)
    inner = coeff * (pre + 0.044715 * pre * pre * pre)
    tanh_val = jnp.tanh(inner)
    value = 0.5 * pre * (1.0 + tanh_val)
    slope = 0.5 * (1.0 + tanh_val) + 0.5 * pre * (1.0 - tanh_val * tanh_val) * coeff * (
        1.0 + 3.0 * 0.044715 * pre * pre
    )
    return (value, slope)


def dot(a, b):
    return jnp.dot(a, b, preferred_element_type=F32)


def dot_nt(a, b):
    return lax.dot_general(a, b, (((1,), (1,)), ((), ())), preferred_element_type=F32)


def dot_tn(a, b):
    return lax.dot_general(a, b, (((0,), (0,)), ((), ())), preferred_element_type=F32)


def norm_pieces(block, gain):
    values = block.astype(F32)
    centred = values - jnp.mean(values, axis=1, keepdims=True)
    inv = lax.rsqrt(jnp.mean(centred * centred, axis=1, keepdims=True) + 1e-06)
    xhat = centred * inv
    return xhat, inv, (xhat * gain[None, :]).astype(BF16)


def slot_ids(routes, experts):
    tok = routes.shape[0]
    eye = jnp.arange(experts, dtype=jnp.int32)
    hot = (routes[:, :, None] == eye).astype(F32)
    named = jnp.sum(hot, axis=1).astype(BF16)
    lower = (jnp.arange(tok)[:, None] > jnp.arange(tok)[None, :]).astype(BF16)
    before = dot(lower, named)
    slot = jnp.sum(before[:, None, :] * hot, axis=2).astype(jnp.int32)
    return routes * 16 + slot


def pack_messages(ids, mixed, cot, experts):
    width = mixed.shape[1]
    half = width // 2
    row = jnp.arange(experts * 8, dtype=jnp.int32)
    main = (row // 8) * 16 + row % 8
    rest = (row // 8) * 16 + 8 + row % 2
    part = (row % 8) // 2
    first, second = ids[:, 0][None, :], ids[:, 1][None, :]
    place = ((main[:, None] == first) | (main[:, None] == second)).astype(BF16)
    late = (rest[:, None] == first) | (rest[:, None] == second)
    late = jnp.concatenate([late & (part == i)[:, None] for i in range(4)], axis=1).astype(BF16)
    source = jnp.concatenate([mixed[:, :half], cot[:, :half], mixed[:, half:], cot[:, half:]], axis=0)
    out = jnp.concatenate([dot(place, mixed), dot(place, cot), dot(late, source)], axis=1)
    return out.astype(BF16).reshape(experts, 8, 2 * width + half)


def unpack_messages(recv, width):
    n = recv.shape[0]
    half = width // 2
    m8 = recv[:, :, :width].reshape(n * 8, width)
    d8 = recv[:, :, width : 2 * width].reshape(n * 8, width)
    rest = recv[:, :, 2 * width :].reshape(n, 4, 2, half)
    m2 = jnp.concatenate([rest[:, 0], rest[:, 2]], axis=-1).reshape(n * 2, width)
    d2 = jnp.concatenate([rest[:, 1], rest[:, 3]], axis=-1).reshape(n * 2, width)
    return jnp.concatenate([m8, m2], axis=0), jnp.concatenate([d8, d2], axis=0)


def expert_pass(rows_m, rows_d, column, w_first, w_second):
    col = column.astype(F32)
    gate = jax.nn.sigmoid(jnp.sum(rows_m.astype(F32) * col[None, :], axis=1, keepdims=True))
    grad_y = (gate * rows_d.astype(F32)).astype(BF16)
    rows = 0.0
    dgate = 0.0
    firsts, seconds = [], []
    for i in range(w_first.shape[0]):
        pre = dot(rows_m, w_first[i])
        value, slope = gelu_parts(pre)
        hidden = value.astype(BF16)
        back = dot_nt(rows_d, w_second[i])
        dgate = dgate + jnp.sum(hidden.astype(F32) * back, axis=1, keepdims=True)
        grad_pre = (gate * back * slope).astype(BF16)
        seconds.append(dot_tn(hidden, grad_y).astype(BF16))
        firsts.append(dot_tn(rows_m, grad_pre).astype(BF16))
        rows = rows + dot_nt(grad_pre, w_first[i])
    coef = dgate * gate * (1.0 - gate)
    rows = rows + coef * col[None, :]
    wide = rows_m.astype(F32)
    sums = jnp.stack([jnp.sum(wide * coef, axis=0), jnp.sum(wide * rows, axis=0)])
    return rows.astype(BF16), sums, jnp.stack(firsts), jnp.stack(seconds)


def body(prenorm_input, gain, router, routes, w_in, w_out, cotangent):
    halves = lax.axis_size("expert")
    experts = halves // 2
    tok, width = prenorm_input.shape
    all_first = lax.all_gather(w_in[0], "dp", axis=0)
    all_second = lax.all_gather(w_out[0], "dp", axis=0)
    xhat, inv, mixed = norm_pieces(prenorm_input, gain)
    ids = slot_ids(routes, experts)
    send = pack_messages(ids, mixed, cotangent, experts)
    send = jnp.repeat(send, 2, axis=0)
    recv = lax.all_to_all(send, "expert", split_axis=0, concat_axis=0, tiled=True)
    rows_m, rows_d = unpack_messages(recv, width)
    own = lax.axis_index("expert") // 2
    column = lax.dynamic_slice_in_dim(router, own, 1, 1)[:, 0]
    rows, sums, firsts, seconds = expert_pass(rows_m, rows_d, column, all_first, all_second)
    grad_in = lax.psum_scatter(firsts, "dp", scatter_dimension=0, tiled=False)[None]
    grad_out = lax.psum_scatter(seconds, "dp", scatter_dimension=0, tiled=False)[None]
    back = jnp.concatenate(
        [
            rows[: halves * 8].reshape(halves, 8, width),
            rows[halves * 8 :].reshape(halves, 2, width),
            jnp.zeros((halves, 6, width), BF16),
        ],
        axis=1,
    )
    ret = lax.all_to_all(back, "expert", split_axis=0, concat_axis=0, tiled=True)
    every = lax.all_gather(sums, ("expert", "dp"), axis=0)
    every = jnp.sum(every.reshape(experts, -1, 2, width), axis=1)
    grad_router = every[:, 0].T
    grad_gain = jnp.sum(every[:, 1], axis=0) / gain
    place = jnp.arange(halves * 16, dtype=jnp.int32)
    place = (place // 32) * 16 + place % 16
    pick = ((ids[:, :1] == place[None, :]) | (ids[:, 1:] == place[None, :])).astype(BF16)
    grad_mixed = dot(pick, ret.reshape(halves * 16, width))
    u = grad_mixed * gain[None, :]
    first = jnp.mean(u, axis=1, keepdims=True)
    second = jnp.mean(u * xhat, axis=1, keepdims=True)
    input_grad = (cotangent.astype(F32) + inv * (u - first - xhat * second)).astype(BF16)
    return (input_grad, grad_in, grad_out, grad_router, grad_gain)


def solution(mesh):
    in_specs = (
        P(("expert", "dp"), None),
        P(),
        P(),
        P(("expert", "dp"), None),
        P("expert", None, "dp"),
        P("expert", "dp", None),
        P(("expert", "dp"), None),
    )
    out_specs = (
        P(("expert", "dp"), None),
        P("expert", None, "dp"),
        P("expert", "dp", None),
        P(),
        P(),
    )
    return jax.shard_map(body, mesh=mesh, in_specs=in_specs, out_specs=out_specs, check_vma=False)
```

time: 644 us -> 352 us (0.55)
  blocking collectives: 226 us -> 0 us
  local copies, waits for them, and re-layouts: 79.3 us -> 22 us
    all_to_all x2 -> x0, blocking collectives: 144 us -> none  [the longest x1 75.7 us: body(): lax.all_to_all(send_m, 'expert', split_axis=0, concat_axis=0, tiled=True)]
    psum x1 -> x0, waiting for transfers between devices: 130 us -> none  [body(): lax.psum((router_term, gain_product), ('expert', 'dp'))]
    all_to_all x2, waiting for transfers between devices: 31.6 us -> 130 us  [the longest x1 73.5 us: body(): lax.all_to_all(send, 'expert', split_axis=0, concat_axis=0, tiled=True)]
    psum x1 -> x0, blocking collectives: 75.6 us -> none  [body(): lax.psum((router_term, gain_product), ('expert', 'dp'))]
    reduce_scatter x1 -> x2, waiting for transfers between devices: 46.7 us -> 84 us  [the longest x1 44.7 us: body(): lax.psum_scatter(firsts, 'dp', scatter_dimension=0, tiled=False)[None]]
    reshape x9 -> x3, local copies, waits for them, and re-layouts: 29 us -> 2.39 us  [the longest x1 1.21 us: unpack_messages(): d8 = recv[:, :, width:2 * width].reshape(n * 8, width)]
    all_gather x2 -> x0, local copies, waits for them, and re-layouts: 22.1 us -> none  [the longest x1 11.2 us: body(): lax.all_gather(recv_m[None], 'dp', axis=0, tiled=True)]
    all_gather x2 -> x3, waiting for transfers between devices: 34.7 us -> 22.9 us  [the longest x1 22.9 us: body(): every = lax.all_gather(sums, ('expert', 'dp'), axis=0)]
  transfers between devices with their start and end apart: 6 -> 7, of which waited for: 4 -> 5; matrix products, arithmetic and copies ran while one was open for 13% -> 17% of each run, Pallas kernels for 0% -> 0%
where the time goes in v1:
time: 352 us; the launch traced here: 351 us
  waiting for transfers between devices  238 us (68%)
  matrix products  37.3 us (11%)
  local copies, waits for them, and re-layouts  22 us (6%)
  starting transfers between devices  20.7 us (6%)
  other arithmetic  18.7 us (5%)
  between operations  14.3 us (4%)
    all_to_all x1, waiting for transfers between devices, body(): lax.all_to_all(send, 'expert', split_axis=0, concat_axis=0, tiled=True)  73.5 us
    all_to_all x1, waiting for transfers between devices, body(): lax.all_to_all(back, 'expert', split_axis=0, concat_axis=0, tiled=True)  56.2 us
    reduce_scatter x1, waiting for transfers between devices, body(): lax.psum_scatter(firsts, 'dp', scatter_dimension=0, tiled=False)[None]  44.7 us
    reduce_scatter x1, waiting for transfers between devices, body(): lax.psum_scatter(seconds, 'dp', scatter_dimension=0, tiled=False)[None]  39.4 us
    all_gather x1, waiting for transfers between devices, body(): every = lax.all_gather(sums, ('expert', 'dp'), axis=0)  22.9 us
    dot_general x8, matrix products, dot_nt(): lax.dot_general(a, b, (((1,), (1,)), ((), ())), preferred_element_type=F32)  15.7 us
    all_to_all x1, starting transfers between devices, body(): lax.all_to_all(send, 'expert', split_axis=0, concat_axis=0, tiled=True)  13.1 us
    dot_general x9, matrix products, dot(): return jnp.dot(a, b, preferred_element_type=F32)  12.4 us
  transfers between devices with their start and end apart: 7, of which 5 were waited for; matrix products, arithmetic and copies ran while one was open for 17% of the time, Pallas kernels for 0%

profile of v1, /device:TPU:1, one launch (start us, length us, event | category | flops | bytes accessed | tf_op | source)
XLA Modules:
  0.0 351.0 jit_solution(10796504383566810328)
XLA Ops:
  9.1 1.2 fusion.63
  12.5 1.2 fusion.57
  16.4 2.0 broadcast_in_dim.4
  18.4 13.1 %all-to-all-start = ((bf16[64,8,3200]{2,1,0:T(8,128)(2,1)}), bf16[64,8,3200]{2,1,0:T(8,128)(2,1)S(1)}, u32[]{:S(2)}, u32[]{:S(2)}) async-start(bf16[64,8,3200]{2,1,0:T(8,128)(2,1)} %bitcast.102), calls=%async_computation | async-start | bytes 6553600 | tf_op jit(solution)/shard_map/all_to_all | solution.py:115
  33.3 73.5 %all-to-all-done = bf16[64,8,3200]{2,1,0:T(8,128)(2,1)S(1)} async-done(((bf16[64,8,3200]{2,1,0:T(8,128)(2,1)}), bf16[64,8,3200]{2,1,0:T(8,128)(2,1)S(1)}, u32[]{:S(2)}, u32[]{:S(2)}) %all-to-all-start) | async-done | bytes 3276832 | tf_op jit(solution)/shard_map/all_to_all | solution.py:115
  108.5 1.6 concatenate.52
  110.1 1.8 copy.47
  111.9 1.6 concatenate.53
  115.3 1.8 copy.44
  117.1 1.6 concatenate.48
  118.7 1.2 slice_bitcast_fusion.1
  121.5 3.5 fusion.54
  124.9 1.7 fusion.55
  126.7 1.7 fusion.56
  128.4 1.7 fusion.53
  130.2 2.6 multiply_reduce_fusion.2
  132.9 1.1 multiply_reduce_fusion.1
  134.2 1.1 multiply_reduce_fusion
  135.5 1.1 multiply_reduce_fusion.3
  139.7 1.1 convolution_add_fusion.1
  140.8 6.4 %fusion.2 = (f32[1280]{0:T(1024)S(1)}, f32[1280]{0:T(1024)S(1)}, bf16[640,1280]{1,0:T(8,128)(2,1)S(1)}) fusion(f32[640]{0:T(1024)S(1)} %subtract_multiply_fusion, bf16[128,640]{1,0:T(8,128)(2,1)S(1)} %concatenate.49, bf16[128,640]{1,0:T(8,128)(2,1)S(1)} %copy-done.10, bf16[512,1280]{1,0:T(8,128)(2,1)S(1)} %copy-done.1, f32[1280]{0:T(1024)S(1)} %convert_reduce_fusion.2, ...), kind=kOutput, calls=%fused_computation.8 | convolution fusion | flops 535754240 | bytes 7804928 | tf_op jit(solution)/shard_map/dot_general | solution.py:28
  148.0 2.8 fusion.5
  154.3 1.9 pad_maximum_fusion.1
  158.2 2.3 maximum_maximum_fusion
  160.5 7.1 %all-to-all-start.1 = ((bf16[64,16,1280]{2,1,0:T(8,128)(2,1)}), bf16[64,16,1280]{2,1,0:T(8,128)(2,1)}, u32[]{:S(2)}, u32[]{:S(2)}) async-start(bf16[64,16,1280]{2,1,0:T(8,128)(2,1)} %maximum_maximum_fusion), calls=%async_computation.1 | async-start | bytes 5242880 | tf_op jit(solution)/shard_map/all_to_all | solution.py:130
  171.5 2.2 pad_maximum_fusion
  173.7 56.2 %all-to-all-done.1 = bf16[64,16,1280]{2,1,0:T(8,128)(2,1)} async-done(((bf16[64,16,1280]{2,1,0:T(8,128)(2,1)}), bf16[64,16,1280]{2,1,0:T(8,128)(2,1)}, u32[]{:S(2)}, u32[]{:S(2)}) %all-to-all-start.1) | async-done | bytes 2621472 | tf_op jit(solution)/shard_map/all_to_all | solution.py:130
  229.9 2.4 fusion.109
  233.4 22.9 %all-gather.10.cloned.1.call-done = f32[256,2,1280]{2,1,0:T(2,128)} async-done(((f32[1,2,1280]{2,1,0:T(2,128)}), f32[256,2,1280]{2,1,0:T(2,128)}) %all-gather.10.cloned.1.call-update) | async-done | bytes 2621456 | tf_op jit(solution)/shard_map/all_gather | solution.py:131
  256.3 2.6 bitcast_reduce_fusion
  260.4 39.4 %reduce-scatter.5.cloned.1.call-done = bf16[1,320,1280]{2,1,0:T(8,128)(2,1)} async-done(((bf16[4,320,1280]{2,1,0:T(8,128)(2,1)}), bf16[1,320,1280]{2,1,0:T(8,128)(2,1)}) %reduce-scatter.5.cloned.1.call-update) | async-done | bytes 819216 | tf_op jit(solution)/shard_map/reduce_scatter | solution.py:121
  299.8 44.7 %reduce-scatter.3.cloned.1.call-done = bf16[1,1280,320]{1,2,0:T(8,128)(2,1)} async-done(((bf16[4,1280,320]{1,2,0:T(8,128)(2,1)}), bf16[1,1280,320]{1,2,0:T(8,128)(2,1)}) %reduce-scatter.3.cloned.1.call-update) | async-done | bytes 819216 | tf_op jit(solution)/shard_map/reduce_scatter | solution.py:120
  (126 shorter events, 29.3 us)
Async XLA Ops:
  7.2 114.3 %all-gather.8.cloned.1.call-start = ((), (), s32[]{:S(2)}) async-start(), calls=%async_computation.5 | async-start | bytes 4096000 | tf_op jit(solution)/shard_map/all_gather | solution.py:109
  12.5 3.3 copy-start.3
  18.4 88.4 %all-to-all-start = ((bf16[64,8,3200]{2,1,0:T(8,128)(2,1)}), bf16[64,8,3200]{2,1,0:T(8,128)(2,1)S(1)}, u32[]{:S(2)}, u32[]{:S(2)}) async-start(bf16[64,8,3200]{2,1,0:T(8,128)(2,1)} %bitcast.102), calls=%async_computation | async-start | bytes 6553600 | tf_op jit(solution)/shard_map/all_to_all | solution.py:115
  31.5 98.6 %all-gather.6.cloned.1.call-start = ((), (), s32[]{:S(2)}) async-start(), calls=%async_computation.4 | async-start | bytes 4096000 | tf_op jit(solution)/shard_map/all_gather | solution.py:110
  32.3 224.0 %all-gather.10.cloned.1.call-start = ((), (), s32[]{:S(2)}) async-start(), calls=%async_computation.8 | async-start | bytes 2631680 | tf_op jit(solution)/shard_map/all_gather | solution.py:131
  118.7 2.3 copy-start.9
  121.4 3.5 %copy-start.1 = (bf16[512,1280]{1,0:T(8,128)(2,1)S(1)}, bf16[512,1280]{1,0:T(8,128)(2,1)}, u32[]{:S(2)}) copy-start(bf16[512,1280]{1,0:T(8,128)(2,1)} %copy-done) | copy-start | bytes 3932164
  121.4 3.5 %copy-start.10 = (bf16[128,640]{1,0:T(8,128)(2,1)S(1)}, bf16[128,640]{1,0:T(8,128)(2,1)}, u32[]{:S(2)}) copy-start(bf16[128,640]{1,0:T(8,128)(2,1)} %concatenate.48) | copy-start | bytes 491524
  121.4 3.5 copy-start.5
  128.4 1.8 copy-start.7
  128.4 1.8 copy-start.18
  128.4 1.8 copy-start.19
  130.2 2.7 copy-start.22
  130.2 2.7 copy-start.27
  132.8 5.7 %copy-start.14 = (bf16[640,320]{0,1:T(8,128)(2,1)}, bf16[640,320]{0,1:T(8,128)(2,1)S(1)}, u32[]{:S(2)}) copy-start(bf16[640,320]{0,1:T(8,128)(2,1)S(1)} %get-tuple-element.13) | copy-start | bytes 1228804
  132.9 1.3 copy-start.25
  134.2 5.5 %copy-start.16 = (bf16[640,320]{0,1:T(8,128)(2,1)}, bf16[640,320]{0,1:T(8,128)(2,1)S(1)}, u32[]{:S(2)}) copy-start(bf16[640,320]{0,1:T(8,128)(2,1)S(1)} %get-tuple-element.17) | copy-start | bytes 1228804
  134.2 1.3 copy-start.23
  135.4 5.4 %copy-start.29 = (bf16[640,320]{0,1:T(8,128)(2,1)}, bf16[640,320]{0,1:T(8,128)(2,1)S(1)}, u32[]{:S(2)}) copy-start(bf16[640,320]{0,1:T(8,128)(2,1)S(1)} %get-tuple-element.19) | copy-start | bytes 1228804
  135.4 2.1 copy-start.6
  136.6 2.0 copy-start.12
  147.9 2.9 copy-start.20
  148.0 151.8 %reduce-scatter.5.cloned.1.call-start = ((), (), s32[]{:S(2)}) async-start(), calls=%async_computation.7 | async-start | bytes 4096000 | tf_op jit(solution)/shard_map/reduce_scatter | solution.py:121
  148.0 2.9 copy-start.8
  148.0 2.9 copy-start.28
  160.5 7.2 %copy-start.11 = (bf16[128,640]{1,0:T(8,128)(2,1)S(1)}, bf16[128,640]{1,0:T(8,128)(2,1)}, u32[]{:S(2)}) copy-start(bf16[128,640]{1,0:T(8,128)(2,1)} %concatenate.48) | copy-start | bytes 491524
  160.5 7.2 %copy-start.13 = (bf16[640,320]{0,1:T(8,128)(2,1)S(1)}, bf16[640,320]{0,1:T(8,128)(2,1)}, u32[]{:S(2)}) copy-start(bf16[640,320]{0,1:T(8,128)(2,1)} %copy-done.12) | copy-start | bytes 1228804
  160.5 69.4 %all-to-all-start.1 = ((bf16[64,16,1280]{2,1,0:T(8,128)(2,1)}), bf16[64,16,1280]{2,1,0:T(8,128)(2,1)}, u32[]{:S(2)}, u32[]{:S(2)}) async-start(bf16[64,16,1280]{2,1,0:T(8,128)(2,1)} %maximum_maximum_fusion), calls=%async_computation.1 | async-start | bytes 5242880 | tf_op jit(solution)/shard_map/all_to_all | solution.py:130
  167.7 176.8 %reduce-scatter.3.cloned.1.call-start = ((), (), s32[]{:S(2)}) async-start(), calls=%async_computation.6 | async-start | bytes 4096000 | tf_op jit(solution)/shard_map/reduce_scatter | solution.py:120
  173.7 56.3 %copy-start.2 = (bf16[128,1280]{1,0:T(8,128)(2,1)S(1)}, bf16[128,1280]{1,0:T(8,128)(2,1)}, u32[]{:S(2)}) copy-start(bf16[128,1280]{1,0:T(8,128)(2,1)} %param.7) | copy-start | bytes 983044
  173.7 56.3 %copy-start.21 = (f32[1280]{0:T(1024)S(1)}, f32[1280]{0:T(1024)}, u32[]{:S(2)}) copy-start(f32[1280]{0:T(1024)} %param.8) | copy-start | bytes 15364
  173.7 58.7 %copy-start.4 = (bf16[128,1280]{1,0:T(8,128)(2,1)S(1)}, bf16[128,1280]{1,0:T(8,128)(2,1)}, u32[]{:S(2)}) copy-start(bf16[128,1280]{1,0:T(8,128)(2,1)} %param.13) | copy-start | bytes 983044
  (6 other events, 6.4 us)
Sparse Core Ops, SparseCore 0:
  9.8 46.7 all-gather.7
  58.3 43.3 all-gather.5
  148.1 108.1 all-gather.9
  259.3 40.4 reduce-scatter.4
  302.8 41.6 reduce-scatter.2

commit v2 on v1

--- a/solution.py
+++ b/solution.py
@@ -1,8 +1,11 @@
+import functools
 import math
 
 import jax
 import jax.numpy as jnp
 from jax import lax
+from jax.experimental import pallas as pl
+from jax.experimental.pallas import tpu as pltpu
 from jax.sharding import PartitionSpec as P
 
 F32 = jnp.float32
@@ -78,46 +81,166 @@
     return jnp.concatenate([m8, m2], axis=0), jnp.concatenate([d8, d2], axis=0)
 
 
-def expert_pass(rows_m, rows_d, column, w_first, w_second):
+def expert_pass(rows_m, rows_d, column, blocks):
     col = column.astype(F32)
     gate = jax.nn.sigmoid(jnp.sum(rows_m.astype(F32) * col[None, :], axis=1, keepdims=True))
     grad_y = (gate * rows_d.astype(F32)).astype(BF16)
     rows = 0.0
     dgate = 0.0
     firsts, seconds = [], []
-    for i in range(w_first.shape[0]):
-        pre = dot(rows_m, w_first[i])
+    for w_first, w_second in blocks:
+        pre = dot_nt(rows_m, w_first)
         value, slope = gelu_parts(pre)
         hidden = value.astype(BF16)
-        back = dot_nt(rows_d, w_second[i])
+        back = dot_nt(rows_d, w_second)
         dgate = dgate + jnp.sum(hidden.astype(F32) * back, axis=1, keepdims=True)
         grad_pre = (gate * back * slope).astype(BF16)
         seconds.append(dot_tn(hidden, grad_y).astype(BF16))
-        firsts.append(dot_tn(rows_m, grad_pre).astype(BF16))
-        rows = rows + dot_nt(grad_pre, w_first[i])
+        firsts.append(dot_tn(grad_pre, rows_m).astype(BF16))
+        rows = rows + dot(grad_pre, w_first)
     coef = dgate * gate * (1.0 - gate)
     rows = rows + coef * col[None, :]
     wide = rows_m.astype(F32)
     sums = jnp.stack([jnp.sum(wide * coef, axis=0), jnp.sum(wide * rows, axis=0)])
-    return rows.astype(BF16), sums, jnp.stack(firsts), jnp.stack(seconds)
+    return rows.astype(BF16), sums, firsts, seconds
+
+
+MESH_ID = pl.DeviceIdType.MESH
+
+
+def dispatch_kernel(chips, groups, send_ref, w_ref, recv_ref, wall_ref, stage, a_send, a_recv, f_send, f_recv, w_send, w_recv, l_sem):
+    me = lax.axis_index("expert")
+    x = lax.axis_index("dp")
+    chip, core = lax.div(me, 2), lax.rem(me, 2)
+    sibling = me + 1 - 2 * core
+    up, down = lax.rem(x + 1, groups), lax.rem(x + groups - 1, groups)
+    barrier = pltpu.get_barrier_semaphore()
+
+    def offset(i):
+        return chips // 2 + lax.div(i + 1, 2) * (1 - 2 * lax.rem(i, 2))
+
+    def greet(i, _):
+        p = lax.rem(chip + offset(i), chips)
+        pl.semaphore_signal(barrier, inc=1, device_id=(2 * p + core, x), device_id_type=MESH_ID)
+        return 0
+
+    lax.fori_loop(0, chips - 1, greet, 0)
+    for peer in ((sibling, x), (me, up), (me, down)):
+        pl.semaphore_signal(barrier, inc=1, device_id=peer, device_id_type=MESH_ID)
+    pl.semaphore_wait(barrier, chips + 2)
+
+    def remote(src, dst, s, r, peer):
+        return pltpu.make_async_remote_copy(
+            src_ref=src, dst_ref=dst, send_sem=s, recv_sem=r, device_id=peer, device_id_type=MESH_ID
+        )
+
+    def weight(src, slot, part, peer):
+        k = 2 * slot + part
+        return remote(src, wall_ref.at[slot, part], w_send.at[k], w_recv.at[k], peer)
+
+    first_in = weight(w_ref.at[0], 0, 0, (me, up))
+    first_out = weight(w_ref.at[1], 2, 1, (me, down))
+    second_out = weight(w_ref.at[1], 0, 1, (me, up))
+    second_in = weight(w_ref.at[0], 2, 0, (me, down))
+    first_in.start()
+    first_out.start()
+
+    def push(i, _):
+        p = lax.rem(chip + offset(i), chips)
+        remote(send_ref.at[p], recv_ref.at[me], a_send.at[i], a_recv.at[i], (2 * p + core, x)).start()
+        return 0
+
+    lax.fori_loop(0, chips - 1, push, 0)
+    second_out.start()
+    second_in.start()
+    mine = remote(send_ref.at[chip], recv_ref.at[me], f_send.at[chips - 1], f_recv.at[chips - 1], (sibling, x))
+    mine.start()
+    load = pltpu.make_async_copy(send_ref.at[chip], stage, l_sem.at[0])
+    load.start()
+    load.wait()
+    keep = pltpu.make_async_copy(stage, recv_ref.at[me], l_sem.at[1])
+    keep.start()
+
+    def relay(i, _):
+        q = 2 * lax.rem(chip - offset(i) + chips, chips) + core
+        remote(send_ref.at[0], recv_ref.at[q], a_send.at[i], a_recv.at[i], (sibling, x)).wait_recv()
+        remote(recv_ref.at[q], recv_ref.at[q], f_send.at[i], f_recv.at[i], (sibling, x)).start()
+        return 0
+
+    lax.fori_loop(0, chips // 2, relay, 0)
+    first_in.wait_recv()
+    third_in = weight(wall_ref.at[0, 0], 1, 0, (me, up))
+    third_in.start()
+    first_out.wait_recv()
+    third_out = weight(wall_ref.at[2, 1], 1, 1, (me, down))
+    third_out.start()
+    lax.fori_loop(chips // 2, chips - 1, relay, 0)
+
+    def finish(i, _):
+        q = 2 * lax.rem(chip - offset(i) + chips, chips) + 1 - core
+        remote(send_ref.at[0], recv_ref.at[0], a_send.at[i], a_recv.at[i], (sibling, x)).wait_send()
+        fwd = remote(recv_ref.at[q], recv_ref.at[q], f_send.at[i], f_recv.at[i], (sibling, x))
+        fwd.wait_send()
+        fwd.wait_recv()
+        return 0
+
+    lax.fori_loop(0, chips - 1, finish, 0)
+    mine.wait_send()
+    remote(send_ref.at[0], recv_ref.at[sibling], f_send.at[chips - 1], f_recv.at[chips - 1], (sibling, x)).wait_recv()
+    keep.wait()
+    second_out.wait_recv()
+    second_in.wait_recv()
+    third_in.wait_recv()
+    third_out.wait_recv()
+    for copy in (first_in, first_out, second_out, second_in, third_in, third_out):
+        copy.wait_send()
+
+
+def dispatch(send, weights, groups):
+    chips = send.shape[0]
+    return pl.pallas_call(
+        functools.partial(dispatch_kernel, chips, groups),
+        out_shape=(
+            jax.ShapeDtypeStruct((2 * chips,) + send.shape[1:], send.dtype),
+            jax.ShapeDtypeStruct((groups - 1,) + weights.shape, weights.dtype),
+        ),
+        in_specs=[pl.BlockSpec(memory_space=pl.ANY)] * 2,
+        out_specs=(pl.BlockSpec(memory_space=pl.ANY),) * 2,
+        scratch_shapes=[
+            pltpu.VMEM(send.shape[1:], send.dtype),
+            pltpu.SemaphoreType.DMA((chips,)),
+            pltpu.SemaphoreType.DMA((chips,)),
+            pltpu.SemaphoreType.DMA((chips,)),
+            pltpu.SemaphoreType.DMA((chips,)),
+            pltpu.SemaphoreType.DMA((6,)),
+            pltpu.SemaphoreType.DMA((6,)),
+            pltpu.SemaphoreType.DMA((2,)),
+        ],
+        compiler_params=pltpu.CompilerParams(collective_id=0, has_side_effects=True),
+        name="dispatch",
+    )(send, weights)
 
 
 def body(prenorm_input, gain, router, routes, w_in, w_out, cotangent):
     halves = lax.axis_size("expert")
     experts = halves // 2
     tok, width = prenorm_input.shape
-    all_first = lax.all_gather(w_in[0], "dp", axis=0)
-    all_second = lax.all_gather(w_out[0], "dp", axis=0)
+    groups = lax.axis_size("dp")
+    weights = jnp.stack([w_in[0].T, w_out[0]])
     xhat, inv, mixed = norm_pieces(prenorm_input, gain)
     ids = slot_ids(routes, experts)
     send = pack_messages(ids, mixed, cotangent, experts)
-    send = jnp.repeat(send, 2, axis=0)
-    recv = lax.all_to_all(send, "expert", split_axis=0, concat_axis=0, tiled=True)
+    recv, others = dispatch(send, weights, groups)
     rows_m, rows_d = unpack_messages(recv, width)
     own = lax.axis_index("expert") // 2
     column = lax.dynamic_slice_in_dim(router, own, 1, 1)[:, 0]
-    rows, sums, firsts, seconds = expert_pass(rows_m, rows_d, column, all_first, all_second)
-    grad_in = lax.psum_scatter(firsts, "dp", scatter_dimension=0, tiled=False)[None]
+    blocks = [(weights[0], weights[1])] + [(others[j, 0], others[j, 1]) for j in range(groups - 1)]
+    rows, sums, firsts, seconds = expert_pass(rows_m, rows_d, column, blocks)
+    here = lax.axis_index("dp")
+    order = lax.rem(here + groups - jnp.arange(groups), groups)
+    firsts = jnp.take(jnp.stack(firsts), order, axis=0)
+    seconds = jnp.take(jnp.stack(seconds), order, axis=0)
+    grad_in = lax.psum_scatter(firsts, "dp", scatter_dimension=0, tiled=False).T[None]
     grad_out = lax.psum_scatter(seconds, "dp", scatter_dimension=0, tiled=False)[None]
     back = jnp.concatenate(
         [

time: 352 us -> 261 us (0.74)
  waiting for transfers between devices: 238 us -> 80.3 us
  Pallas kernels: 0 us -> 67.2 us
  starting transfers between devices: 20.7 us -> 6.24 us
  other arithmetic: 18.7 us -> 27.3 us
  matrix products: 37.3 us -> 41.9 us
    all_to_all x1 -> x0, waiting for transfers between devices: 73.5 us -> none  [body(): lax.all_to_all(send, 'expert', split_axis=0, concat_axis=0, tiled=True)]
    pallas_call x0 -> x1, Pallas kernels: none -> 67.2 us  [dispatch(): pl.pallas_call(functools.partial(dispatch_kernel, chips, groups), out_sha...]
    reduce_scatter x1, waiting for transfers between devices: 44.7 us -> 0.01 us  [body(): lax.psum_scatter(firsts, 'dp', scatter_dimension=0, tiled=False).T[None]]
    reduce_scatter x1, waiting for transfers between devices: 39.4 us -> 0.01 us  [body(): lax.psum_scatter(seconds, 'dp', scatter_dimension=0, tiled=False)[None]]
    all_to_all x1 -> x0, starting transfers between devices: 13.1 us -> none  [body(): lax.all_to_all(send, 'expert', split_axis=0, concat_axis=0, tiled=True)]
    gather x0 -> x2, local copies, waits for them, and re-layouts: none -> 7.12 us  [the longest x1 4.39 us: body(): firsts = jnp.take(jnp.stack(firsts), order, axis=0)]
    all_to_all x1, waiting for transfers between devices: 56.2 us -> 63.3 us  [body(): lax.all_to_all(back, 'expert', split_axis=0, concat_axis=0, tiled=True)]
    all_gather x1, waiting for transfers between devices: 22.9 us -> 16.5 us  [body(): every = lax.all_gather(sums, ('expert', 'dp'), axis=0)]
  transfers between devices with their start and end apart: 7 -> 4, of which waited for: 5 -> 2; matrix products, arithmetic and copies ran while one was open for 17% -> 13% of each run, Pallas kernels for 0% -> 0%
where the time goes in v2:
time: 261 us; the launch traced here: 260 us
  waiting for transfers between devices  80.3 us (31%)
  Pallas kernels  67.2 us (26%)
  matrix products  41.9 us (16%)
  other arithmetic  27.3 us (10%)
  local copies, waits for them, and re-layouts  20.7 us (8%)
  between operations  16.2 us (6%)
  starting transfers between devices  6.24 us (2%)
    pallas_call x1, Pallas kernels, dispatch(): pl.pallas_call(functools.partial(dispatch_kernel, chips, groups), out_sha...  67.2 us
    all_to_all x1, waiting for transfers between devices, body(): lax.all_to_all(back, 'expert', split_axis=0, concat_axis=0, tiled=True)  63.3 us
    dot_general x8, matrix products, dot_nt(): lax.dot_general(a, b, (((1,), (1,)), ((), ())), preferred_element_type=F32)  19 us
    all_gather x1, waiting for transfers between devices, body(): every = lax.all_gather(sums, ('expert', 'dp'), axis=0)  16.5 us
    dot_general x9, matrix products, dot(): return jnp.dot(a, b, preferred_element_type=F32)  12.5 us
    dot_general x8, matrix products, dot_tn(): lax.dot_general(a, b, (((0,), (0,)), ((), ())), preferred_element_type=F32)  10.4 us
    all_to_all x1, starting transfers between devices, body(): lax.all_to_all(back, 'expert', split_axis=0, concat_axis=0, tiled=True)  6.11 us
    select_n x1, other arithmetic, body(): seconds = jnp.take(jnp.stack(seconds), order, axis=0)  5.23 us
  transfers between devices with their start and end apart: 4, of which 2 were waited for; matrix products, arithmetic and copies ran while one was open for 13% of the time, Pallas kernels for 0%

profile of v2, /device:TPU:1, one launch (start us, length us, event | category | flops | bytes accessed | tf_op | source)
XLA Modules:
  0.0 259.8 jit_solution(5161394818658664960)
XLA Ops:
  8.1 1.2 convert_reduce_fusion
  9.4 1.2 fusion.84
  12.8 1.2 fusion.78
  15.9 1.3 pad_maximum_fusion.3.w_ref
  17.8 1.4 pad_maximum_fusion.2.send_ref
  19.2 67.2 %dispatch.1 = (bf16[64,8,3200]{2,1,0:T(8,128)(2,1)}, bf16[3,2,320,1280]{3,2,1,0:T(8,128)(2,1)}) custom-call(bf16[32,8,3200]{2,1,0:T(8,128)(2,1)} %pad_maximum_fusion.2.send_ref, bf16[2,320,1280]{2,1,0:T(8,128)(2,1)} %pad_maximum_fusion.3.w_ref), custom_call_target="tpu_custom_call" | custom-call | tf_op jit(solution)/shard_map/dispatch/pallas_call | solution.py:201
  87.6 3.0 %slice_bitcast_fusion.1 = (bf16[512,1280]{1,0:T(8,128)(2,1)}, bf16[512,1280]{1,0:T(8,128)(2,1)S(1)}) fusion(bf16[64,8,3200]{2,1,0:T(8,128)(2,1)} %get-tuple-element.8), kind=kLoop, calls=%fused_computation.45 | loop fusion | bytes 5242880 | tf_op jit(solution)/shard_map/reshape | solution.py:77
  90.9 1.2 fusion.132
  92.2 3.0 %fusion.54 = f32[640,320]{0,1:T(8,128)} fusion(bf16[3,2,320,1280]{3,2,1,0:T(8,128)(2,1)} %get-tuple-element.9, bf16[128,640]{1,0:T(8,128)(2,1)S(1)} %concatenate.49, bf16[128,640]{1,0:T(8,128)(2,1)S(1)} %concatenate.48, bf16[512,1280]{1,0:T(8,128)(2,1)S(1)} %get-tuple-element.16), kind=kOutput, calls=%fused_computation.96 | convolution fusion | flops 529203200 | bytes 3276800 | tf_op jit(solution)/shard_map/dot_general | solution.py:31
  95.2 2.9 %fusion.49 = f32[640,320]{0,1:T(8,128)} fusion(bf16[3,2,320,1280]{3,2,1,0:T(8,128)(2,1)} %get-tuple-element.9, bf16[128,640]{1,0:T(8,128)(2,1)S(1)} %concatenate.49, bf16[128,640]{1,0:T(8,128)(2,1)S(1)} %concatenate.48, bf16[512,1280]{1,0:T(8,128)(2,1)S(1)} %get-tuple-element.16), kind=kOutput, calls=%fused_computation.91 | convolution fusion | flops 529203200 | bytes 3276800 | tf_op jit(solution)/shard_map/dot_general | solution.py:31
  98.0 2.9 %fusion.44 = f32[640,320]{0,1:T(8,128)} fusion(bf16[3,2,320,1280]{3,2,1,0:T(8,128)(2,1)} %get-tuple-element.9, bf16[128,640]{1,0:T(8,128)(2,1)S(1)} %concatenate.49, bf16[128,640]{1,0:T(8,128)(2,1)S(1)} %concatenate.48, bf16[512,1280]{1,0:T(8,128)(2,1)S(1)} %get-tuple-element.16), kind=kOutput, calls=%fused_computation.86 | convolution fusion | flops 529203200 | bytes 3276800 | tf_op jit(solution)/shard_map/dot_general | solution.py:31
  100.9 2.8 %fusion.60 = f32[640,320]{0,1:T(8,128)} fusion(bf16[1,1280,320]{1,2,0:T(8,128)(2,1)S(1)} %copy-done.3, bf16[128,640]{1,0:T(8,128)(2,1)} %copy-done.10, bf16[128,640]{1,0:T(8,128)(2,1)} %copy-done.13, bf16[512,1280]{1,0:T(8,128)(2,1)S(1)} %get-tuple-element.16), kind=kOutput, calls=%fused_computation.102 | convolution fusion | flops 529203200 | bytes 3276800 | tf_op jit(solution)/shard_map/dot_general | solution.py:31
  103.8 1.7 concatenate.52
  106.2 1.4 fusion.1
  107.6 1.7 concatenate.53
  109.2 2.8 %multiply_reduce_fusion.2 = (f32[640]{0:T(1024)S(1)}, bf16[640,320]{0,1:T(8,128)(2,1)S(1)}) fusion(f32[640,320]{0,1:T(8,128)} %fusion.54, f32[640]{0:T(1024)S(1)} %add_divide_fusion, bf16[3,2,320,1280]{3,2,1,0:T(8,128)(2,1)} %get-tuple-element.9, bf16[128,640]{1,0:T(8,128)(2,1)} %concatenate.53, bf16[128,640]{1,0:T(8,128)(2,1)} %concatenate.52, ...), kind=kOutput, calls=%fused_computation.110 | convolution fusion | flops 534322560 | bytes 3691520 | tf_op jit(solution)/shard_map/dot_general | solution.py:31
  112.1 2.4 multiply_reduce_fusion.1
  119.4 1.1 convolution_add_fusion.1
  120.7 7.3 %fusion.2 = (f32[1280]{0:T(1024)S(1)}, f32[1280]{0:T(1024)S(1)}, bf16[640,1280]{1,0:T(8,128)(2,1)}) fusion(f32[640]{0:T(1024)S(1)} %subtract_multiply_fusion, bf16[128,640]{1,0:T(8,128)(2,1)S(1)} %copy-done.11, bf16[128,640]{1,0:T(8,128)(2,1)S(1)} %copy-done.14, bf16[512,1280]{1,0:T(8,128)(2,1)S(1)} %get-tuple-element.16, ...), kind=kOutput, calls=%fused_computation.10 | convolution fusion | flops 535754240 | bytes 7804928 | tf_op jit(solution)/shard_map/dot_general | solution.py:27
  128.7 2.3 fusion.9
  134.4 2.0 pad_maximum_fusion.1
  136.4 2.7 %gather_fusion.1 = bf16[4,320,1280]{2,1,0:T(8,128)(2,1)S(1)} fusion(bf16[4,320,1280]{2,1,0:T(8,128)(2,1)} %pad_maximum_fusion.1, s32[1024]{0:T(1024)S(1)} %pad_clamp_fusion), kind=kCustom, calls=%fused_computation.1.clone | custom fusion | bytes 6553616 | tf_op jit(solution)/shard_map/jit(_take)/gather | solution.py:242
  139.2 2.5 fusion.4
  144.5 2.0 pad_maximum_fusion
  146.4 4.4 %gather_fusion = bf16[4,320,1280]{2,1,0:T(8,128)(2,1)} fusion(bf16[4,320,1280]{2,1,0:T(8,128)(2,1)} %pad_maximum_fusion, s32[1024]{0:T(1024)S(1)} %pad_clamp_fusion), kind=kCustom, calls=%fused_computation.clone | custom fusion | bytes 6553616 | tf_op jit(solution)/shard_map/jit(_take)/gather | solution.py:241
  150.8 5.2 %broadcast_select_fusion = (bf16[4,320,1280]{2,1,0:T(8,128)(2,1)}, bf16[4,320,1280]{2,1,0:T(8,128)(2,1)}) fusion(bf16[4,320,1280]{2,1,0:T(8,128)(2,1)S(1)} %gather_fusion.1, pred[4]{0:T(512)(128)(4,1)S(1)} %compare_and_fusion, bf16[4,320,1280]{2,1,0:T(8,128)(2,1)} %gather_fusion), kind=kLoop, calls=%fused_computation.15 | loop fusion | flops 3276800 | bytes 13107204 | tf_op jit(solution)/shard_map/jit(_take)/select_n | solution.py:242
  156.1 1.4 copy-done.6
  157.8 2.2 maximum_maximum_fusion
  160.0 6.1 %all-to-all-start = ((bf16[64,16,1280]{2,1,0:T(8,128)(2,1)}), bf16[64,16,1280]{2,1,0:T(8,128)(2,1)S(1)}, u32[]{:S(2)}, u32[]{:S(2)}) async-start(bf16[64,16,1280]{2,1,0:T(8,128)(2,1)} %maximum_maximum_fusion), calls=%async_computation | async-start | bytes 5242880 | tf_op jit(solution)/shard_map/all_to_all | solution.py:253
  166.7 63.3 %all-to-all-done = bf16[64,16,1280]{2,1,0:T(8,128)(2,1)S(1)} async-done(((bf16[64,16,1280]{2,1,0:T(8,128)(2,1)}), bf16[64,16,1280]{2,1,0:T(8,128)(2,1)S(1)}, u32[]{:S(2)}, u32[]{:S(2)}) %all-to-all-start) | async-done | bytes 2621472 | tf_op jit(solution)/shard_map/all_to_all | solution.py:253
  231.8 16.5 %all-gather.4.cloned.1.call-done = f32[256,2,1280]{2,1,0:T(2,128)} async-done(((f32[1,2,1280]{2,1,0:T(2,128)}), f32[256,2,1280]{2,1,0:T(2,128)}) %all-gather.4.cloned.1.call-update) | async-done | bytes 2621456 | tf_op jit(solution)/shard_map/all_gather | solution.py:254
  248.3 2.6 bitcast_reduce_fusion
  (132 shorter events, 22.9 us)
Async XLA Ops:
  8.0 7.5 %copy-start.4 = (bf16[128,1280]{1,0:T(8,128)(2,1)S(1)}, bf16[128,1280]{1,0:T(8,128)(2,1)}, u32[]{:S(2)}) copy-start(bf16[128,1280]{1,0:T(8,128)(2,1)} %param.15) | copy-start | bytes 983044
  8.0 7.9 %copy-start.8 = (bf16[1,320,1280]{2,1,0:T(8,128)(2,1)S(1)}, bf16[1,320,1280]{2,1,0:T(8,128)(2,1)}, u32[]{:S(2)}) copy-start(bf16[1,320,1280]{2,1,0:T(8,128)(2,1)} %param.14) | copy-start | bytes 2457604
  8.0 7.9 %copy-start.3 = (bf16[1,1280,320]{1,2,0:T(8,128)(2,1)S(1)}, bf16[1,1280,320]{1,2,0:T(8,128)(2,1)}, u32[]{:S(2)}) copy-start(bf16[1,1280,320]{1,2,0:T(8,128)(2,1)} %param.13) | copy-start | bytes 2457604
  8.0 240.2 %all-gather.4.cloned.1.call-start = ((), (), s32[]{:S(2)}) async-start(), calls=%async_computation.5 | async-start | bytes 2631680 | tf_op jit(solution)/shard_map/all_gather | solution.py:254
  90.6 30.0 %copy-start = (bf16[512,1280]{1,0:T(8,128)(2,1)}, bf16[512,1280]{1,0:T(8,128)(2,1)S(1)}, u32[]{:S(2)}) copy-start(bf16[512,1280]{1,0:T(8,128)(2,1)S(1)} %get-tuple-element.16) | copy-start | bytes 3932164
  92.1 5.9 %copy-start.10 = (bf16[128,640]{1,0:T(8,128)(2,1)}, bf16[128,640]{1,0:T(8,128)(2,1)S(1)}, u32[]{:S(2)}) copy-start(bf16[128,640]{1,0:T(8,128)(2,1)S(1)} %concatenate.49) | copy-start | bytes 491524
  92.2 5.8 %copy-start.13 = (bf16[128,640]{1,0:T(8,128)(2,1)}, bf16[128,640]{1,0:T(8,128)(2,1)S(1)}, u32[]{:S(2)}) copy-start(bf16[128,640]{1,0:T(8,128)(2,1)S(1)} %concatenate.48) | copy-start | bytes 491524
  100.9 8.3 %copy-start.7 = (bf16[512,1280]{1,0:T(8,128)(2,1)S(1)}, bf16[512,1280]{1,0:T(8,128)(2,1)}, u32[]{:S(2)}) copy-start(bf16[512,1280]{1,0:T(8,128)(2,1)} %get-tuple-element.15) | copy-start | bytes 3932164
  109.2 2.8 %copy-start.21 = (bf16[128,640]{1,0:T(8,128)(2,1)S(1)}, bf16[128,640]{1,0:T(8,128)(2,1)}, u32[]{:S(2)}) copy-start(bf16[128,640]{1,0:T(8,128)(2,1)} %concatenate.52) | copy-start | bytes 491524
  109.2 2.8 %copy-start.23 = (bf16[128,640]{1,0:T(8,128)(2,1)S(1)}, bf16[128,640]{1,0:T(8,128)(2,1)}, u32[]{:S(2)}) copy-start(bf16[128,640]{1,0:T(8,128)(2,1)} %concatenate.53) | copy-start | bytes 491524
  109.2 2.8 %copy-start.30 = (f32[640,320]{0,1:T(8,128)S(1)}, f32[640,320]{0,1:T(8,128)}, u32[]{:S(2)}) copy-start(f32[640,320]{0,1:T(8,128)} %fusion.49) | copy-start | bytes 2457604
  109.2 5.3 %slice-start = ((s8[4915200]{0:T(1024)(128)(4,1)}), s8[4194304]{0:T(1024)(128)(4,1)S(1)}, s32[]{:S(2)}) async-start(s8[4915200]{0:T(1024)(128)(4,1)} %bitcast.107), calls=%async_computation.6 | async-start | bytes 8388608
  112.1 6.3 %copy-start.17 = (bf16[640,320]{0,1:T(8,128)(2,1)}, bf16[640,320]{0,1:T(8,128)(2,1)S(1)}, u32[]{:S(2)}) copy-start(bf16[640,320]{0,1:T(8,128)(2,1)S(1)} %get-tuple-element.18) | copy-start | bytes 1228804
  112.1 2.5 slice-start.1
  112.1 2.5 copy-start.28
  114.6 4.8 %copy-start.19 = (bf16[640,320]{0,1:T(8,128)(2,1)}, bf16[640,320]{0,1:T(8,128)(2,1)S(1)}, u32[]{:S(2)}) copy-start(bf16[640,320]{0,1:T(8,128)(2,1)S(1)} %get-tuple-element.22) | copy-start | bytes 1228804
  114.6 1.5 copy-start.26
  116.1 4.5 %copy-start.32 = (bf16[640,320]{0,1:T(8,128)(2,1)}, bf16[640,320]{0,1:T(8,128)(2,1)S(1)}, u32[]{:S(2)}) copy-start(bf16[640,320]{0,1:T(8,128)(2,1)S(1)} %get-tuple-element.24) | copy-start | bytes 1228804
  120.6 8.1 %copy-start.22 = (bf16[128,640]{1,0:T(8,128)(2,1)S(1)}, bf16[128,640]{1,0:T(8,128)(2,1)}, u32[]{:S(2)}) copy-start(bf16[128,640]{1,0:T(8,128)(2,1)} %concatenate.52) | copy-start | bytes 491524
  120.6 8.1 %copy-start.24 = (bf16[128,640]{1,0:T(8,128)(2,1)S(1)}, bf16[128,640]{1,0:T(8,128)(2,1)}, u32[]{:S(2)}) copy-start(bf16[128,640]{1,0:T(8,128)(2,1)} %concatenate.53) | copy-start | bytes 491524
  128.6 123.8 %reduce-scatter.5.cloned.1.call-start = ((), (), s32[]{:S(2)}) async-start(), calls=%async_computation.4 | async-start | bytes 4096000 | tf_op jit(solution)/shard_map/reduce_scatter | solution.py:244
  128.7 2.3 copy-start.31
  136.4 2.7 %copy-start.12 = (bf16[128,640]{1,0:T(8,128)(2,1)S(1)}, bf16[128,640]{1,0:T(8,128)(2,1)}, u32[]{:S(2)}) copy-start(bf16[128,640]{1,0:T(8,128)(2,1)} %copy-done.10) | copy-start | bytes 491524
  139.1 2.5 copy-start.1
  139.1 2.5 copy-start.15
  139.1 2.5 copy-start.33
  156.1 1.4 copy-start.6
  160.0 70.0 %copy-start.2 = (bf16[128,1280]{1,0:T(8,128)(2,1)S(1)}, bf16[128,1280]{1,0:T(8,128)(2,1)}, u32[]{:S(2)}) copy-start(bf16[128,1280]{1,0:T(8,128)(2,1)} %param.9) | copy-start | bytes 983044
  160.0 70.0 %copy-start.25 = (f32[1280]{0:T(1024)S(1)}, f32[1280]{0:T(1024)}, u32[]{:S(2)}) copy-start(f32[1280]{0:T(1024)} %param.10) | copy-start | bytes 15364
  160.0 70.0 %all-to-all-start = ((bf16[64,16,1280]{2,1,0:T(8,128)(2,1)}), bf16[64,16,1280]{2,1,0:T(8,128)(2,1)S(1)}, u32[]{:S(2)}, u32[]{:S(2)}) async-start(bf16[64,16,1280]{2,1,0:T(8,128)(2,1)} %maximum_maximum_fusion), calls=%async_computation | async-start | bytes 5242880 | tf_op jit(solution)/shard_map/all_to_all | solution.py:253
  166.1 86.3 %reduce-scatter.3.cloned.1.call-start = ((), (), s32[]{:S(2)}) async-start(), calls=%async_computation.3 | async-start | bytes 4096000 | tf_op jit(solution)/shard_map/reduce_scatter | solution.py:243
  166.2 64.5 %copy-start.5 = (bf16[128,1280]{1,0:T(8,128)(2,1)S(1)}, bf16[128,1280]{1,0:T(8,128)(2,1)}, u32[]{:S(2)}) copy-start(bf16[128,1280]{1,0:T(8,128)(2,1)} %param.15) | copy-start | bytes 983044
  (8 other events, 9.1 us)
Sparse Core Ops, SparseCore 0:
  128.7 119.4 all-gather.3
Sparse Core Ops, SparseCore 1:
  156.2 37.2 reduce-scatter.4
  196.5 43.8 reduce-scatter.2

commit v3 on v2

--- a/solution.py
+++ b/solution.py
@@ -219,6 +219,137 @@
         compiler_params=pltpu.CompilerParams(collective_id=0, has_side_effects=True),
         name="dispatch",
     )(send, weights)
+
+
+def collect_kernel(chips, groups, back_ref, sums_ref, ret_ref, mine, other, total, extra, gsum, o_send, o_recv, s_send, s_recv, r_send, r_recv, l_sem, k_sem):
+    me = lax.axis_index("expert")
+    x = lax.axis_index("dp")
+    chip, core = lax.div(me, 2), lax.rem(me, 2)
+    sibling = me + 1 - 2 * core
+    team = 2 * groups
+    seat = 2 * x + core
+    barrier = pltpu.get_barrier_semaphore()
+
+    def offset(i):
+        return chips // 2 + lax.div(i + 1, 2) * (1 - 2 * lax.rem(i, 2))
+
+    def mate(d):
+        k = lax.rem(seat + d, team)
+        return (2 * chip + lax.rem(k, 2), lax.div(k, 2))
+
+    def greet(i, _):
+        p = lax.rem(chip + offset(i), chips)
+        pl.semaphore_signal(barrier, inc=1, device_id=(2 * p + core, x), device_id_type=MESH_ID)
+        return 0
+
+    lax.fori_loop(0, chips - 1, greet, 0)
+    for d in range(1, team):
+        pl.semaphore_signal(barrier, inc=1, device_id=mate(d), device_id_type=MESH_ID)
+    pl.semaphore_wait(barrier, chips + team - 2)
+
+    def remote(src, dst, s, r, peer):
+        return pltpu.make_async_remote_copy(
+            src_ref=src, dst_ref=dst, send_sem=s, recv_sem=r, device_id=peer, device_id_type=MESH_ID
+        )
+
+    def share(d, slot):
+        return remote(sums_ref, gsum.at[slot], s_send.at[d], s_recv.at[d], mate(d))
+
+    def swap(i):
+        p = lax.rem(chip + offset(i), chips)
+        return remote(back_ref.at[p, 1 - core], other.at[i], o_send.at[i], o_recv.at[i], (sibling, x))
+
+    def load(i):
+        p = lax.rem(chip + offset(i), chips)
+        return pltpu.make_async_copy(back_ref.at[p, core], mine.at[i], l_sem.at[i])
+
+    for d in range(1, team):
+        share(d, seat).start()
+    own_sums = pltpu.make_async_copy(sums_ref, gsum.at[seat], k_sem.at[0])
+    own_sums.start()
+
+    def fetch(i, _):
+        swap(i).start()
+        load(i).start()
+        return 0
+
+    lax.fori_loop(0, chips, fetch, 0)
+    own_sums.wait()
+    for d in range(1, team):
+        share(d, lax.rem(seat + team - d, team)).wait_recv()
+    whole = gsum[0]
+    for j in range(1, team):
+        whole = whole + gsum[j]
+    row = lax.broadcasted_iota(jnp.int32, extra.shape, 0)
+    placed = jnp.zeros(extra.shape, F32)
+    for part in range(3):
+        piece = whole.astype(BF16).astype(F32)
+        whole = whole - piece
+        for j in range(2):
+            placed = placed + jnp.where(row == 10 + 2 * part + j, piece[j : j + 1], 0.0)
+    extra[...] = placed
+
+    def add(i):
+        load(i).wait()
+        swap(i).wait_recv()
+        total[i] = (mine[i].astype(F32) + other[i].astype(F32) + extra[...]).astype(BF16)
+
+    def give(i, slot):
+        p = lax.rem(chip + offset(i), chips)
+        return remote(total.at[i], ret_ref.at[slot], r_send.at[i], r_recv.at[i], (2 * p + core, x))
+
+    add(0)
+
+    def step(i, _):
+        add(i)
+        give(i - 1, chip).start()
+        return 0
+
+    lax.fori_loop(1, chips, step, 0)
+    keep = pltpu.make_async_copy(total.at[chips - 1], ret_ref.at[chip], k_sem.at[1])
+    keep.start()
+
+    def finish(i, _):
+        q = lax.rem(chip - offset(i) + chips, chips)
+        copy = give(i, q)
+        copy.wait_send()
+        copy.wait_recv()
+        swap(i).wait_send()
+        return 0
+
+    lax.fori_loop(0, chips - 1, finish, 0)
+    swap(chips - 1).wait_send()
+    keep.wait()
+    for d in range(1, team):
+        share(d, seat).wait_send()
+
+
+def collect(back, sums, groups):
+    chips, _, slots, width = back.shape
+    block = (chips, slots, width)
+    return pl.pallas_call(
+        functools.partial(collect_kernel, chips, groups),
+        out_shape=jax.ShapeDtypeStruct(block, back.dtype),
+        in_specs=[pl.BlockSpec(memory_space=pl.ANY)] * 2,
+        out_specs=pl.BlockSpec(memory_space=pl.ANY),
+        scratch_shapes=[
+            pltpu.VMEM(block, back.dtype),
+            pltpu.VMEM(block, back.dtype),
+            pltpu.VMEM(block, back.dtype),
+            pltpu.VMEM((slots, width), F32),
+            pltpu.VMEM((2 * groups,) + sums.shape, F32),
+            pltpu.SemaphoreType.DMA((chips,)),
+            pltpu.SemaphoreType.DMA((chips,)),
+            pltpu.SemaphoreType.DMA((2 * groups,)),
+            pltpu.SemaphoreType.DMA((2 * groups,)),
+            pltpu.SemaphoreType.DMA((chips,)),
+            pltpu.SemaphoreType.DMA((chips,)),
+            pltpu.SemaphoreType.DMA((chips,)),
+            pltpu.SemaphoreType.DMA((2,)),
+        ],
+        compiler_params=pltpu.CompilerParams(collective_id=1, has_side_effects=True),
+        name="collect",
+    )(back, sums)
 
 
 def body(prenorm_input, gain, router, routes, w_in, w_out, cotangent):
@@ -250,15 +381,13 @@
         ],
         axis=1,
     )
-    ret = lax.all_to_all(back, "expert", split_axis=0, concat_axis=0, tiled=True)
-    every = lax.all_gather(sums, ("expert", "dp"), axis=0)
-    every = jnp.sum(every.reshape(experts, -1, 2, width), axis=1)
+    ret = collect(back.reshape(experts, 2, 16, width), sums, groups)
+    every = ret[:, 10:12].astype(F32) + ret[:, 12:14].astype(F32) + ret[:, 14:].astype(F32)
     grad_router = every[:, 0].T
     grad_gain = jnp.sum(every[:, 1], axis=0) / gain
-    place = jnp.arange(halves * 16, dtype=jnp.int32)
-    place = (place // 32) * 16 + place % 16
+    place = jnp.arange(experts * 16, dtype=jnp.int32)
     pick = ((ids[:, :1] == place[None, :]) | (ids[:, 1:] == place[None, :])).astype(BF16)
-    grad_mixed = dot(pick, ret.reshape(halves * 16, width))
+    grad_mixed = dot(pick, ret.reshape(experts * 16, width))
     u = grad_mixed * gain[None, :]
     first = jnp.mean(u, axis=1, keepdims=True)
     second = jnp.mean(u * xhat, axis=1, keepdims=True)

time: 261 us -> 223 us (0.85)
  waiting for transfers between devices: 80.3 us -> 20.6 us
  Pallas kernels: 67.2 us -> 110 us
  matrix products: 41.9 us -> 33.5 us
  starting transfers between devices: 6.24 us -> 0.08 us
  local copies, waits for them, and re-layouts: 20.7 us -> 15.3 us
    all_to_all x1 -> x0, waiting for transfers between devices: 63.3 us -> none  [body(): lax.all_to_all(back, 'expert', split_axis=0, concat_axis=0, tiled=True)]
    pallas_call x0 -> x1, Pallas kernels: none -> 42.8 us  [collect(): pl.pallas_call(functools.partial(collect_kernel, chips, groups), out_shap...]
    reduce_scatter x1, waiting for transfers between devices: 0.01 us -> 19.9 us  [body(): lax.psum_scatter(firsts, 'dp', scatter_dimension=0, tiled=False).T[None]]
    all_gather x1 -> x0, waiting for transfers between devices: 16.5 us -> none  [body(): every = lax.all_gather(sums, ('expert', 'dp'), axis=0)]
    dot_general x8, matrix products: 19 us -> 10.3 us  [dot_nt(): lax.dot_general(a, b, (((1,), (1,)), ((), ())), preferred_element_type=F32)]
    all_to_all x1 -> x0, starting transfers between devices: 6.11 us -> none  [body(): lax.all_to_all(back, 'expert', split_axis=0, concat_axis=0, tiled=True)]
    concatenate x2, local copies, waits for them, and re-layouts: 3.31 us -> 0.13 us  [unpack_messages(): jnp.concatenate([rest[:, 1], rest[:, 3]], axis=-1).reshape(n * 2, width)]
  transfers between devices with their start and end apart: 4 -> 2, of which waited for: 2 -> 1; matrix products, arithmetic and copies ran while one was open for 13% -> 8% of each run, Pallas kernels for 0% -> 19%
where the time goes in v3:
time: 223 us; the launch traced here: 222 us
  Pallas kernels  110 us (49%)
  matrix products  33.5 us (15%)
  other arithmetic  27.6 us (12%)
  waiting for transfers between devices  20.6 us (9%)
  local copies, waits for them, and re-layouts  15.3 us (7%)
  between operations  14.7 us (7%)
    pallas_call x1, Pallas kernels, dispatch(): pl.pallas_call(functools.partial(dispatch_kernel, chips, groups), out_sha...  67.2 us
    pallas_call x1, Pallas kernels, collect(): pl.pallas_call(functools.partial(collect_kernel, chips, groups), out_shap...  42.8 us
    reduce_scatter x1, waiting for transfers between devices, body(): lax.psum_scatter(firsts, 'dp', scatter_dimension=0, tiled=False).T[None]  19.9 us
    dot_general x9, matrix products, dot(): return jnp.dot(a, b, preferred_element_type=F32)  11.7 us
    dot_general x8, matrix products, dot_tn(): lax.dot_general(a, b, (((0,), (0,)), ((), ())), preferred_element_type=F32)  11.5 us
    dot_general x8, matrix products, dot_nt(): lax.dot_general(a, b, (((1,), (1,)), ((), ())), preferred_element_type=F32)  10.3 us
    select_n x1, other arithmetic, body(): seconds = jnp.take(jnp.stack(seconds), order, axis=0)  5.35 us
    gather x1, local copies, waits for them, and re-layouts, body(): firsts = jnp.take(jnp.stack(firsts), order, axis=0)  4.49 us
  transfers between devices with their start and end apart: 2, of which 1 were waited for; matrix products, arithmetic and copies ran while one was open for 8% of the time, Pallas kernels for 19%

profile of v3, /device:TPU:1, one launch (start us, length us, event | category | flops | bytes accessed | tf_op | source)
XLA Modules:
  0.0 221.8 jit_solution(6148111389095764051)
XLA Ops:
  7.3 1.2 convert_reduce_fusion
  8.6 1.2 fusion.84
  12.0 1.2 fusion.78
  15.1 1.3 pad_maximum_fusion.3.w_ref
  17.0 1.4 pad_maximum_fusion.2.send_ref
  18.4 67.2 %dispatch.1 = (bf16[64,8,3200]{2,1,0:T(8,128)(2,1)}, bf16[3,2,320,1280]{3,2,1,0:T(8,128)(2,1)}) custom-call(bf16[32,8,3200]{2,1,0:T(8,128)(2,1)} %pad_maximum_fusion.2.send_ref, bf16[2,320,1280]{2,1,0:T(8,128)(2,1)} %pad_maximum_fusion.3.w_ref), custom_call_target="tpu_custom_call" | custom-call | tf_op jit(solution)/shard_map/dispatch/pallas_call | solution.py:201
  85.6 1.1 slice.87
  86.8 3.0 %slice_bitcast_fusion = (bf16[512,1280]{1,0:T(8,128)(2,1)}, bf16[512,1280]{1,0:T(8,128)(2,1)S(1)}) fusion(bf16[64,8,3200]{2,1,0:T(8,128)(2,1)} %get-tuple-element.8), kind=kLoop, calls=%fused_computation.43 | loop fusion | bytes 5242880 | tf_op jit(solution)/shard_map/reshape | solution.py:77
  92.1 2.1 fusion.54
  94.2 2.3 %multiply_reduce_fusion.2 = (f32[640]{0:T(1024)S(1)}, bf16[640,320]{0,1:T(8,128)(2,1)S(1)}) fusion(f32[640,320]{0,1:T(8,128)S(1)} %fusion.54, f32[640]{0:T(1024)S(1)} %add_divide_fusion, bf16[3,2,320,1280]{3,2,1,0:T(8,128)(2,1)} %get-tuple-element.9, bf16[128,640]{1,0:T(8,128)(2,1)S(1)} %concatenate.58, bf16[128,640]{1,0:T(8,128)(2,1)S(1)} %concatenate.57, ...), kind=kOutput, calls=%fused_computation.108 | convolution fusion | flops 534322560 | bytes 3691520 | tf_op jit(solution)/shard_map/dot_general | solution.py:31
  98.6 1.1 multiply_reduce_fusion.1
  99.7 1.1 fusion.10
  101.7 1.1 multiply_reduce_fusion
  105.1 1.1 multiply_reduce_fusion.3
  106.2 1.1 fusion.8
  107.3 2.0 fusion.4
  109.3 1.7 fusion.7
  111.0 1.7 fusion.6
  112.7 1.8 fusion.5
  114.5 1.9 pad_maximum_fusion.1
  116.3 2.7 %gather_fusion.1 = bf16[4,320,1280]{2,1,0:T(8,128)(2,1)S(1)} fusion(bf16[4,320,1280]{2,1,0:T(8,128)(2,1)} %pad_maximum_fusion.1, s32[1024]{0:T(1024)S(1)} %pad_clamp_fusion), kind=kCustom, calls=%fused_computation.1.clone | custom fusion | bytes 6553616 | tf_op jit(solution)/shard_map/jit(_take)/gather | solution.py:373
  119.0 3.3 %pad_maximum_fusion = bf16[4,320,1280]{2,1,0:T(8,128)(2,1)} fusion(bf16[1,320,1280]{2,1,0:T(8,128)(2,1)} %fusion.7, bf16[1,320,1280]{2,1,0:T(8,128)(2,1)} %fusion.6, bf16[1,320,1280]{2,1,0:T(8,128)(2,1)} %fusion.5, bf16[1,320,1280]{2,1,0:T(8,128)(2,1)} %fusion.4), kind=kLoop, calls=%fused_computation.12 | loop fusion | flops 4915200 | bytes 6553600 | tf_op jit(solution)/shard_map/stack | solution.py:372
  122.3 4.5 %gather_fusion = bf16[4,320,1280]{2,1,0:T(8,128)(2,1)} fusion(bf16[4,320,1280]{2,1,0:T(8,128)(2,1)} %pad_maximum_fusion, s32[1024]{0:T(1024)S(1)} %pad_clamp_fusion), kind=kCustom, calls=%fused_computation.clone | custom fusion | bytes 6553616 | tf_op jit(solution)/shard_map/jit(_take)/gather | solution.py:372
  126.8 5.3 %broadcast_select_fusion = (bf16[4,320,1280]{2,1,0:T(8,128)(2,1)}, bf16[4,320,1280]{2,1,0:T(8,128)(2,1)}) fusion(bf16[4,320,1280]{2,1,0:T(8,128)(2,1)S(1)} %gather_fusion.1, pred[4]{0:T(512)(128)(4,1)S(1)} %compare_and_fusion, bf16[4,320,1280]{2,1,0:T(8,128)(2,1)} %gather_fusion), kind=kLoop, calls=%fused_computation.15 | loop fusion | flops 3276800 | bytes 13107204 | tf_op jit(solution)/shard_map/jit(_take)/select_n | solution.py:373
  134.4 2.2 %convolution_add_fusion.2 = f32[640,1280]{1,0:T(8,128)S(1)} fusion(f32[640,1280]{1,0:T(8,128)S(1)} %fusion.62, bf16[640,320]{0,1:T(8,128)(2,1)S(1)} %copy-done.15, bf16[3,2,320,1280]{3,2,1,0:T(8,128)(2,1)} %get-tuple-element.9), kind=kOutput, calls=%fused_computation.8 | convolution fusion | flops 525107200 | bytes 7782400 | tf_op jit(solution)/shard_map/dot_general | solution.py:27
  136.7 2.4 %convolution_add_fusion.1 = f32[640,1280]{1,0:T(8,128)S(1)} fusion(f32[640,1280]{1,0:T(8,128)S(1)} %convolution_add_fusion.2, bf16[640,320]{0,1:T(8,128)(2,1)S(1)} %copy-done.17, bf16[3,2,320,1280]{3,2,1,0:T(8,128)(2,1)} %get-tuple-element.9), kind=kOutput, calls=%fused_computation.7 | convolution fusion | flops 525107200 | bytes 7782400 | tf_op jit(solution)/shard_map/dot_general | solution.py:27
  139.2 2.9 %fusion.2 = (f32[1280]{0:T(1024)S(1)}, f32[1280]{0:T(1024)S(1)}, bf16[640,1280]{1,0:T(8,128)(2,1)S(1)}) fusion(f32[640]{0:T(1024)S(1)} %subtract_multiply_fusion, bf16[128,640]{1,0:T(8,128)(2,1)S(1)} %concatenate.54, bf16[128,640]{1,0:T(8,128)(2,1)S(1)} %copy-done.11, bf16[512,1280]{1,0:T(8,128)(2,1)S(1)} %copy-done.1, f32[1280]{0:T(1024)S(1)} %convert_reduce_fusion.2, ...), kind=kOutput, calls=%fused_computation.10 | convolution fusion | flops 535754240 | bytes 7800320 | tf_op jit(solution)/shard_map/dot_general | solution.py:27
  143.1 2.2 %maximum_maximum_fusion.back_ref = bf16[32,2,16,1280]{3,2,1,0:T(8,128)(2,1)} fusion(bf16[32,2,2,1280]{3,2,1,0:T(2,128)(2,1)S(1)} %concatenate.62, bf16[32,2,8,1280]{3,2,1,0:T(8,128)(2,1)S(1)} %bitcast.100, bf16[16]{0:T(256)(128)(2,1)S(1)} %pad.12.clone), kind=kLoop, calls=%fused_computation.25 | loop fusion | flops 7864320 | bytes 4259872 | tf_op jit(solution)/shard_map/concatenate | solution.py:376
  145.3 42.8 %collect.1 = bf16[32,16,1280]{2,1,0:T(8,128)(2,1)} custom-call(bf16[32,2,16,1280]{3,2,1,0:T(8,128)(2,1)} %maximum_maximum_fusion.back_ref, f32[2,1280]{1,0:T(2,128)} %pad_maximum_fusion.4.sums_ref), custom_call_target="tpu_custom_call" | custom-call | tf_op jit(solution)/shard_map/collect/pallas_call | solution.py:330
  188.1 2.4 %convert_add_fusion = f32[32,2,1280]{2,1,0:T(2,128)S(1)} fusion(bf16[32,16,1280]{2,1,0:T(8,128)(2,1)} %collect.1), kind=kLoop, calls=%fused_computation.149 | loop fusion | flops 409600 | bytes 819200 | tf_op jit(solution)/shard_map/add | solution.py:385
  192.1 1.8 fusion.119
  195.0 19.9 %reduce-scatter.3.cloned.1.call-done = bf16[1,320,1280]{2,1,0:T(8,128)(2,1)} async-done(((bf16[4,320,1280]{2,1,0:T(8,128)(2,1)}), bf16[1,320,1280]{2,1,0:T(8,128)(2,1)}) %reduce-scatter.3.cloned.1.call-update) | async-done | bytes 819216 | tf_op jit(solution)/shard_map/reduce_scatter | solution.py:374
  (105 shorter events, 17.9 us)
Async XLA Ops:
  7.2 7.5 %copy-start.5 = (bf16[128,1280]{1,0:T(8,128)(2,1)S(1)}, bf16[128,1280]{1,0:T(8,128)(2,1)}, u32[]{:S(2)}) copy-start(bf16[128,1280]{1,0:T(8,128)(2,1)} %param.15) | copy-start | bytes 983044
  7.2 7.9 %copy-start.8 = (bf16[1,320,1280]{2,1,0:T(8,128)(2,1)S(1)}, bf16[1,320,1280]{2,1,0:T(8,128)(2,1)}, u32[]{:S(2)}) copy-start(bf16[1,320,1280]{2,1,0:T(8,128)(2,1)} %param.14) | copy-start | bytes 2457604
  7.2 7.9 %copy-start.3 = (bf16[1,1280,320]{1,2,0:T(8,128)(2,1)S(1)}, bf16[1,1280,320]{1,2,0:T(8,128)(2,1)}, u32[]{:S(2)}) copy-start(bf16[1,1280,320]{1,2,0:T(8,128)(2,1)} %param.13) | copy-start | bytes 2457604
  7.2 187.8 %reduce-scatter.5.cloned.1.call-start = ((), (), s32[]{:S(2)}) async-start(), calls=%async_computation.3 | async-start | bytes 4096000 | tf_op jit(solution)/shard_map/reduce_scatter | solution.py:375
  89.8 22.9 %copy-start = (bf16[512,1280]{1,0:T(8,128)(2,1)}, bf16[512,1280]{1,0:T(8,128)(2,1)S(1)}, u32[]{:S(2)}) copy-start(bf16[512,1280]{1,0:T(8,128)(2,1)S(1)} %get-tuple-element.16) | copy-start | bytes 3932164
  90.7 22.0 %copy-start.10 = (bf16[128,640]{1,0:T(8,128)(2,1)}, bf16[128,640]{1,0:T(8,128)(2,1)S(1)}, u32[]{:S(2)}) copy-start(bf16[128,640]{1,0:T(8,128)(2,1)S(1)} %concatenate.53) | copy-start | bytes 491524
  92.0 4.5 %copy-start.18 = (bf16[128,640]{1,0:T(8,128)(2,1)}, bf16[128,640]{1,0:T(8,128)(2,1)S(1)}, u32[]{:S(2)}) copy-start(bf16[128,640]{1,0:T(8,128)(2,1)S(1)} %concatenate.58) | copy-start | bytes 491524
  92.0 2.2 copy-start.7
  92.1 5.6 %slice-start = ((s8[4915200]{0:T(1024)(128)(4,1)}), s8[4194304]{0:T(1024)(128)(4,1)S(1)}, s32[]{:S(2)}) async-start(s8[4915200]{0:T(1024)(128)(4,1)} %bitcast.103), calls=%async_computation.4 | async-start | bytes 8388608
  94.2 3.5 %slice-start.1 = ((s8[4915200]{0:T(1024)(128)(4,1)}), s8[720896]{0:T(1024)(128)(4,1)S(1)}, s32[]{:S(2)}) async-start(s8[4915200]{0:T(1024)(128)(4,1)} %bitcast.103), calls=%async_computation.5 | async-start | bytes 1441792
  96.6 16.1 %copy-start.14 = (bf16[640,320]{0,1:T(8,128)(2,1)}, bf16[640,320]{0,1:T(8,128)(2,1)S(1)}, u32[]{:S(2)}) copy-start(bf16[640,320]{0,1:T(8,128)(2,1)S(1)} %get-tuple-element.18) | copy-start | bytes 1228804
  97.7 0.9 copy-start.19
  99.7 11.3 %copy-start.16 = (bf16[640,320]{0,1:T(8,128)(2,1)}, bf16[640,320]{0,1:T(8,128)(2,1)S(1)}, u32[]{:S(2)}) copy-start(bf16[640,320]{0,1:T(8,128)(2,1)S(1)} %get-tuple-element.22) | copy-start | bytes 1228804
  102.8 6.5 %copy-start.21 = (bf16[640,320]{0,1:T(8,128)(2,1)}, bf16[640,320]{0,1:T(8,128)(2,1)S(1)}, u32[]{:S(2)}) copy-start(bf16[640,320]{0,1:T(8,128)(2,1)S(1)} %get-tuple-element.24) | copy-start | bytes 1228804
  103.9 1.1 copy-start.9
  106.2 1.1 copy-start.12
  132.1 1.1 copy-start.4
  132.1 1.2 copy-start.13
  132.2 82.8 %reduce-scatter.3.cloned.1.call-start = ((), (), s32[]{:S(2)}) async-start(), calls=%async_computation.2 | async-start | bytes 4096000 | tf_op jit(solution)/shard_map/reduce_scatter | solution.py:374
  132.2 2.2 %copy-start.15 = (bf16[640,320]{0,1:T(8,128)(2,1)S(1)}, bf16[640,320]{0,1:T(8,128)(2,1)}, u32[]{:S(2)}) copy-start(bf16[640,320]{0,1:T(8,128)(2,1)} %copy-done.14) | copy-start | bytes 1228804
  134.4 2.3 %copy-start.17 = (bf16[640,320]{0,1:T(8,128)(2,1)S(1)}, bf16[640,320]{0,1:T(8,128)(2,1)}, u32[]{:S(2)}) copy-start(bf16[640,320]{0,1:T(8,128)(2,1)} %copy-done.16) | copy-start | bytes 1228804
  136.7 2.5 %copy-start.1 = (bf16[512,1280]{1,0:T(8,128)(2,1)S(1)}, bf16[512,1280]{1,0:T(8,128)(2,1)}, u32[]{:S(2)}) copy-start(bf16[512,1280]{1,0:T(8,128)(2,1)} %copy-done) | copy-start | bytes 3932164
  136.7 2.5 %copy-start.11 = (bf16[128,640]{1,0:T(8,128)(2,1)S(1)}, bf16[128,640]{1,0:T(8,128)(2,1)}, u32[]{:S(2)}) copy-start(bf16[128,640]{1,0:T(8,128)(2,1)} %copy-done.10) | copy-start | bytes 491524
  136.7 2.5 %copy-start.22 = (bf16[640,320]{0,1:T(8,128)(2,1)S(1)}, bf16[640,320]{0,1:T(8,128)(2,1)}, u32[]{:S(2)}) copy-start(bf16[640,320]{0,1:T(8,128)(2,1)} %copy-done.21) | copy-start | bytes 1228804
  145.3 45.5 %copy-start.20 = (f32[1280]{0:T(1024)S(1)}, f32[1280]{0:T(1024)}, u32[]{:S(2)}) copy-start(f32[1280]{0:T(1024)} %param.10) | copy-start | bytes 15364
  145.3 46.8 %copy-start.2 = (bf16[128,1280]{1,0:T(8,128)(2,1)S(1)}, bf16[128,1280]{1,0:T(8,128)(2,1)}, u32[]{:S(2)}) copy-start(bf16[128,1280]{1,0:T(8,128)(2,1)} %param.9) | copy-start | bytes 983044
  145.3 48.6 %copy-start.6 = (bf16[128,1280]{1,0:T(8,128)(2,1)S(1)}, bf16[128,1280]{1,0:T(8,128)(2,1)}, u32[]{:S(2)}) copy-start(bf16[128,1280]{1,0:T(8,128)(2,1)} %param.15) | copy-start | bytes 983044
Sparse Core Ops, SparseCore 0:
  132.3 37.7 reduce-scatter.4
  173.2 41.6 reduce-scatter.2

commit v4 on v3

--- a/solution.py
+++ b/solution.py
@@ -369,8 +369,8 @@
     rows, sums, firsts, seconds = expert_pass(rows_m, rows_d, column, blocks)
     here = lax.axis_index("dp")
     order = lax.rem(here + groups - jnp.arange(groups), groups)
-    firsts = jnp.take(jnp.stack(firsts), order, axis=0)
-    seconds = jnp.take(jnp.stack(seconds), order, axis=0)
+    firsts = jnp.take(jnp.stack(firsts), order, axis=0, mode="clip")
+    seconds = jnp.take(jnp.stack(seconds), order, axis=0, mode="clip")
     grad_in = lax.psum_scatter(firsts, "dp", scatter_dimension=0, tiled=False).T[None]
     grad_out = lax.psum_scatter(seconds, "dp", scatter_dimension=0, tiled=False)[None]
     back = jnp.concatenate(

time: 223 us -> 206 us (0.924)
  waiting for transfers between devices: 20.6 us -> 0.59 us
  other arithmetic: 27.6 us -> 19 us
  matrix products: 33.5 us -> 41.1 us
  local copies, waits for them, and re-layouts: 15.3 us -> 19.5 us
    reduce_scatter x1, waiting for transfers between devices: 19.9 us -> 0.56 us  [body(): lax.psum_scatter(firsts, 'dp', scatter_dimension=0, tiled=False).T[None]]
    dot_general x8, matrix products: 10.3 us -> 20.8 us  [dot_nt(): lax.dot_general(a, b, (((1,), (1,)), ((), ())), preferred_element_type=F32)]
    select_n x2 -> x0, other arithmetic: 5.36 us -> none  [the longest x1 5.35 us: body(): seconds = jnp.take(jnp.stack(seconds), order, axis=0)]
    another operation x2, other arithmetic: 5.12 us -> 1.14 us  [the longest x1 0.68 us: body(): firsts = jnp.take(jnp.stack(firsts), order, axis=0, mode='clip')]
    unnamed x51 -> x75, local copies, waits for them, and re-layouts: 1.59 us -> 5.38 us
    dot_general x8, matrix products: 11.5 us -> 8.7 us  [dot_tn(): lax.dot_general(a, b, (((0,), (0,)), ((), ())), preferred_element_type=F32)]
  transfers between devices with their start and end apart: 2 -> 2, of which waited for: 1 -> 1; matrix products, arithmetic and copies ran while one was open for 8% -> 17% of each run, Pallas kernels for 19% -> 21%
where the time goes in v4:
time: 206 us; the launch traced here: 205 us
  Pallas kernels  110 us (53%)
  matrix products  41.1 us (20%)
  local copies, waits for them, and re-layouts  19.5 us (9%)
  other arithmetic  19 us (9%)
  between operations  14.7 us (7%)
    pallas_call x1, Pallas kernels, dispatch(): pl.pallas_call(functools.partial(dispatch_kernel, chips, groups), out_sha...  67.2 us
    pallas_call x1, Pallas kernels, collect(): pl.pallas_call(functools.partial(collect_kernel, chips, groups), out_shap...  42.5 us
    dot_general x8, matrix products, dot_nt(): lax.dot_general(a, b, (((1,), (1,)), ((), ())), preferred_element_type=F32)  20.8 us
    dot_general x9, matrix products, dot(): return jnp.dot(a, b, preferred_element_type=F32)  11.6 us
    dot_general x8, matrix products, dot_tn(): lax.dot_general(a, b, (((0,), (0,)), ((), ())), preferred_element_type=F32)  8.7 us
    unnamed x75, local copies, waits for them, and re-layouts  5.38 us
  transfers between devices with their start and end apart: 2, of which 1 were waited for; matrix products, arithmetic and copies ran while one was open for 17% of the time, Pallas kernels for 21%

profile of v4, /device:TPU:1, one launch (start us, length us, event | category | flops | bytes accessed | tf_op | source)
XLA Modules:
  0.0 205.0 jit_solution(13093800479516889070)
XLA Ops:
  7.3 1.2 convert_reduce_fusion
  8.5 1.2 fusion.84
  12.0 1.2 fusion.78
  13.2 1.1 fusion.122
  15.1 1.3 pad_maximum_fusion.3.w_ref
  17.0 1.4 pad_maximum_fusion.2.send_ref
  18.4 67.2 %dispatch.1 = (bf16[64,8,3200]{2,1,0:T(8,128)(2,1)}, bf16[3,2,320,1280]{3,2,1,0:T(8,128)(2,1)}) custom-call(bf16[32,8,3200]{2,1,0:T(8,128)(2,1)} %pad_maximum_fusion.2.send_ref, bf16[2,320,1280]{2,1,0:T(8,128)(2,1)} %pad_maximum_fusion.3.w_ref), custom_call_target="tpu_custom_call" | custom-call | tf_op jit(solution)/shard_map/dispatch/pallas_call | solution.py:201
  85.6 1.1 slice.87
  86.7 3.1 %slice_bitcast_fusion = (bf16[512,1280]{1,0:T(8,128)(2,1)}, bf16[512,1280]{1,0:T(8,128)(2,1)S(1)}) fusion(bf16[64,8,3200]{2,1,0:T(8,128)(2,1)} %get-tuple-element.7), kind=kLoop, calls=%fused_computation.41 | loop fusion | bytes 5242880 | tf_op jit(solution)/shard_map/reshape | solution.py:77
  90.0 1.2 fusion.121
  91.4 2.9 %fusion.54 = f32[640,320]{0,1:T(8,128)} fusion(bf16[3,2,320,1280]{3,2,1,0:T(8,128)(2,1)} %get-tuple-element.8, bf16[128,640]{1,0:T(8,128)(2,1)S(1)} %concatenate.54, bf16[128,640]{1,0:T(8,128)(2,1)S(1)} %concatenate.53, bf16[512,1280]{1,0:T(8,128)(2,1)S(1)} %get-tuple-element.15), kind=kOutput, calls=%fused_computation.92 | convolution fusion | flops 529203200 | bytes 3276800 | tf_op jit(solution)/shard_map/dot_general | solution.py:31
  94.3 2.9 %fusion.49 = f32[640,320]{0,1:T(8,128)} fusion(bf16[3,2,320,1280]{3,2,1,0:T(8,128)(2,1)} %get-tuple-element.8, bf16[128,640]{1,0:T(8,128)(2,1)S(1)} %concatenate.54, bf16[128,640]{1,0:T(8,128)(2,1)S(1)} %concatenate.53, bf16[512,1280]{1,0:T(8,128)(2,1)S(1)} %get-tuple-element.15), kind=kOutput, calls=%fused_computation.87 | convolution fusion | flops 529203200 | bytes 3276800 | tf_op jit(solution)/shard_map/dot_general | solution.py:31
  97.2 2.9 %fusion.44 = f32[640,320]{0,1:T(8,128)} fusion(bf16[3,2,320,1280]{3,2,1,0:T(8,128)(2,1)} %get-tuple-element.8, bf16[128,640]{1,0:T(8,128)(2,1)S(1)} %concatenate.54, bf16[128,640]{1,0:T(8,128)(2,1)S(1)} %concatenate.53, bf16[512,1280]{1,0:T(8,128)(2,1)S(1)} %get-tuple-element.15), kind=kOutput, calls=%fused_computation.82 | convolution fusion | flops 529203200 | bytes 3276800 | tf_op jit(solution)/shard_map/dot_general | solution.py:31
  100.1 2.9 %fusion.60 = f32[640,320]{0,1:T(8,128)} fusion(bf16[1,1280,320]{1,2,0:T(8,128)(2,1)S(1)} %copy-done.4, bf16[128,640]{1,0:T(8,128)(2,1)} %copy-done.12, bf16[128,640]{1,0:T(8,128)(2,1)} %copy-done.15, bf16[512,1280]{1,0:T(8,128)(2,1)S(1)} %get-tuple-element.15), kind=kOutput, calls=%fused_computation.98 | convolution fusion | flops 529203200 | bytes 3276800 | tf_op jit(solution)/shard_map/dot_general | solution.py:31
  104.8 1.4 fusion.1
  107.2 2.3 %fusion.9 = bf16[1,320,1280]{2,1,0:T(8,128)(2,1)S(1)} fusion(f32[640,320]{0,1:T(8,128)} %fusion.54, f32[640]{0:T(1024)S(1)} %add_divide_fusion, bf16[128,640]{1,0:T(8,128)(2,1)S(1)} %concatenate.58, bf16[128,640]{1,0:T(8,128)(2,1)S(1)} %concatenate.57, bf16[512,1280]{1,0:T(8,128)(2,1)S(1)} %copy-done.8), kind=kOutput, calls=%fused_computation.31 | convolution fusion | flops 533094400 | bytes 3279360 | tf_op jit(solution)/shard_map/dot_general | solution.py:35
  109.5 1.1 fusion.10
  111.8 1.1 fusion.8
  113.4 2.5 %gather_fusion.1 = bf16[4,320,1280]{2,1,0:T(8,128)(2,1)} fusion(bf16[4,320,1280]{2,1,0:T(8,128)(2,1)S(1)} %pad_maximum_fusion.1, s32[1024]{0:T(1024)S(1)} %pad_clamp_fusion), kind=kCustom, calls=%fused_computation.1 | custom fusion | bytes 6553616 | tf_op jit(solution)/shard_map/jit(_take)/gather | solution.py:373
  117.4 2.4 %multiply_reduce_fusion.3 = (f32[640]{0:T(1024)S(1)}, bf16[640,320]{0,1:T(8,128)(2,1)S(1)}) fusion(f32[640,320]{0,1:T(8,128)} %fusion.60, f32[640]{0:T(1024)S(1)} %add_divide_fusion, bf16[1,320,1280]{2,1,0:T(8,128)(2,1)S(1)} %copy-done.11, bf16[128,640]{1,0:T(8,128)(2,1)} %copy-done.26, bf16[128,640]{1,0:T(8,128)(2,1)} %copy-done.24, ...), kind=kOutput, calls=%fused_computation.108 | convolution fusion | flops 534322560 | bytes 3691520 | tf_op jit(solution)/shard_map/dot_general | solution.py:31
  121.4 2.3 %multiply_reduce_fusion = (f32[640]{0:T(1024)S(1)}, bf16[640,320]{0,1:T(8,128)(2,1)S(1)}) fusion(f32[640,320]{0,1:T(8,128)S(1)} %copy-done.34, f32[640]{0:T(1024)S(1)} %add_divide_fusion, bf16[3,2,320,1280]{3,2,1,0:T(8,128)(2,1)} %get-tuple-element.8, bf16[128,640]{1,0:T(8,128)(2,1)S(1)} %copy-done.27, bf16[128,640]{1,0:T(8,128)(2,1)S(1)} %copy-done.25, ...), kind=kOutput, calls=%fused_computation.102 | convolution fusion | flops 534322560 | bytes 3691520 | tf_op jit(solution)/shard_map/dot_general | solution.py:31
  125.3 2.3 %multiply_reduce_fusion.1 = (f32[640]{0:T(1024)S(1)}, bf16[640,320]{0,1:T(8,128)(2,1)S(1)}) fusion(f32[640,320]{0,1:T(8,128)S(1)} %copy-done.32, f32[640]{0:T(1024)S(1)} %add_divide_fusion, bf16[3,2,320,1280]{3,2,1,0:T(8,128)(2,1)} %get-tuple-element.8, bf16[128,640]{1,0:T(8,128)(2,1)S(1)} %copy-done.27, bf16[128,640]{1,0:T(8,128)(2,1)S(1)} %copy-done.25, ...), kind=kOutput, calls=%fused_computation.104 | convolution fusion | flops 534322560 | bytes 3691520 | tf_op jit(solution)/shard_map/dot_general | solution.py:31
  128.9 2.3 %multiply_reduce_fusion.2 = (f32[640]{0:T(1024)S(1)}, bf16[640,320]{0,1:T(8,128)(2,1)S(1)}) fusion(f32[640,320]{0,1:T(8,128)S(1)} %copy-done.30, f32[640]{0:T(1024)S(1)} %add_divide_fusion, bf16[3,2,320,1280]{3,2,1,0:T(8,128)(2,1)} %get-tuple-element.8, bf16[128,640]{1,0:T(8,128)(2,1)S(1)} %copy-done.27, bf16[128,640]{1,0:T(8,128)(2,1)S(1)} %copy-done.25, ...), kind=kOutput, calls=%fused_computation.106 | convolution fusion | flops 534322560 | bytes 3691520 | tf_op jit(solution)/shard_map/dot_general | solution.py:31
  132.7 2.6 %gather_fusion = bf16[4,320,1280]{2,1,0:T(8,128)(2,1)} fusion(bf16[4,320,1280]{2,1,0:T(8,128)(2,1)S(1)} %pad_maximum_fusion, s32[1024]{0:T(1024)S(1)} %pad_clamp_fusion), kind=kCustom, calls=%fused_computation | custom fusion | bytes 6553616 | tf_op jit(solution)/shard_map/jit(_take)/gather | solution.py:372
  135.3 1.1 copy-done.5
  137.6 2.2 %convolution_add_fusion.2 = f32[640,1280]{1,0:T(8,128)S(1)} fusion(f32[640,1280]{1,0:T(8,128)S(1)} %fusion.62, bf16[640,320]{0,1:T(8,128)(2,1)S(1)} %copy-done.23, bf16[3,2,320,1280]{3,2,1,0:T(8,128)(2,1)} %get-tuple-element.8), kind=kOutput, calls=%fused_computation.8 | convolution fusion | flops 525107200 | bytes 7782400 | tf_op jit(solution)/shard_map/dot_general | solution.py:27
  139.9 2.4 %convolution_add_fusion.1 = f32[640,1280]{1,0:T(8,128)S(1)} fusion(f32[640,1280]{1,0:T(8,128)S(1)} %convolution_add_fusion.2, bf16[640,320]{0,1:T(8,128)(2,1)S(1)} %copy-done.21, bf16[3,2,320,1280]{3,2,1,0:T(8,128)(2,1)} %get-tuple-element.8), kind=kOutput, calls=%fused_computation.7 | convolution fusion | flops 525107200 | bytes 7782400 | tf_op jit(solution)/shard_map/dot_general | solution.py:27
  142.4 2.8 %fusion.2 = (f32[1280]{0:T(1024)S(1)}, f32[1280]{0:T(1024)S(1)}, bf16[640,1280]{1,0:T(8,128)(2,1)S(1)}) fusion(f32[640]{0:T(1024)S(1)} %subtract_multiply_fusion, bf16[128,640]{1,0:T(8,128)(2,1)S(1)} %copy-done.14, bf16[128,640]{1,0:T(8,128)(2,1)S(1)} %copy-done.17, bf16[512,1280]{1,0:T(8,128)(2,1)S(1)} %copy-done.2, f32[1280]{0:T(1024)S(1)} %convert_reduce_fusion.2, ...), kind=kOutput, calls=%fused_computation.10 | convolution fusion | flops 535754240 | bytes 7800320 | tf_op jit(solution)/shard_map/dot_general | solution.py:27
  146.2 2.3 %maximum_maximum_fusion.back_ref = bf16[32,2,16,1280]{3,2,1,0:T(8,128)(2,1)} fusion(bf16[32,2,2,1280]{3,2,1,0:T(2,128)(2,1)S(1)} %concatenate.62, bf16[32,2,8,1280]{3,2,1,0:T(8,128)(2,1)S(1)} %bitcast.102, bf16[16]{0:T(256)(128)(2,1)S(1)} %pad.12.clone), kind=kLoop, calls=%fused_computation.23 | loop fusion | flops 7864320 | bytes 4259872 | tf_op jit(solution)/shard_map/concatenate | solution.py:376
  148.4 42.5 %collect.1 = bf16[32,16,1280]{2,1,0:T(8,128)(2,1)} custom-call(bf16[32,2,16,1280]{3,2,1,0:T(8,128)(2,1)} %maximum_maximum_fusion.back_ref, f32[2,1280]{1,0:T(2,128)} %pad_maximum_fusion.4.sums_ref), custom_call_target="tpu_custom_call" | custom-call | tf_op jit(solution)/shard_map/collect/pallas_call | solution.py:330
  191.0 2.2 %convert_add_fusion = f32[32,2,1280]{2,1,0:T(2,128)S(1)} fusion(bf16[32,16,1280]{2,1,0:T(8,128)(2,1)} %collect.1), kind=kLoop, calls=%fused_computation.147 | loop fusion | flops 409600 | bytes 819200 | tf_op jit(solution)/shard_map/add | solution.py:385
  194.7 1.8 fusion.120
  (126 shorter events, 21.3 us)
Async XLA Ops:
  7.2 7.5 %copy-start.6 = (bf16[128,1280]{1,0:T(8,128)(2,1)S(1)}, bf16[128,1280]{1,0:T(8,128)(2,1)}, u32[]{:S(2)}) copy-start(bf16[128,1280]{1,0:T(8,128)(2,1)} %param.13) | copy-start | bytes 983044
  7.2 7.9 %copy-start.10 = (bf16[1,320,1280]{2,1,0:T(8,128)(2,1)S(1)}, bf16[1,320,1280]{2,1,0:T(8,128)(2,1)}, u32[]{:S(2)}) copy-start(bf16[1,320,1280]{2,1,0:T(8,128)(2,1)} %param.12) | copy-start | bytes 2457604
  7.2 7.9 %copy-start.4 = (bf16[1,1280,320]{1,2,0:T(8,128)(2,1)S(1)}, bf16[1,1280,320]{1,2,0:T(8,128)(2,1)}, u32[]{:S(2)}) copy-start(bf16[1,1280,320]{1,2,0:T(8,128)(2,1)} %param.11) | copy-start | bytes 2457604
  7.2 190.4 %reduce-scatter.5.cloned.1.call-start = ((), (), s32[]{:S(2)}) async-start(), calls=%async_computation.3 | async-start | bytes 4096000 | tf_op jit(solution)/shard_map/reduce_scatter | solution.py:375
  89.8 15.0 %copy-start = (bf16[512,1280]{1,0:T(8,128)(2,1)}, bf16[512,1280]{1,0:T(8,128)(2,1)S(1)}, u32[]{:S(2)}) copy-start(bf16[512,1280]{1,0:T(8,128)(2,1)S(1)} %get-tuple-element.15) | copy-start | bytes 3932164
  91.3 5.9 %copy-start.12 = (bf16[128,640]{1,0:T(8,128)(2,1)}, bf16[128,640]{1,0:T(8,128)(2,1)S(1)}, u32[]{:S(2)}) copy-start(bf16[128,640]{1,0:T(8,128)(2,1)S(1)} %concatenate.54) | copy-start | bytes 491524
  91.4 5.8 %copy-start.15 = (bf16[128,640]{1,0:T(8,128)(2,1)}, bf16[128,640]{1,0:T(8,128)(2,1)S(1)}, u32[]{:S(2)}) copy-start(bf16[128,640]{1,0:T(8,128)(2,1)S(1)} %concatenate.53) | copy-start | bytes 491524
  100.1 7.1 %copy-start.8 = (bf16[512,1280]{1,0:T(8,128)(2,1)S(1)}, bf16[512,1280]{1,0:T(8,128)(2,1)}, u32[]{:S(2)}) copy-start(bf16[512,1280]{1,0:T(8,128)(2,1)} %get-tuple-element.14) | copy-start | bytes 3932164
  104.0 7.8 %copy-start.24 = (bf16[128,640]{1,0:T(8,128)(2,1)}, bf16[128,640]{1,0:T(8,128)(2,1)S(1)}, u32[]{:S(2)}) copy-start(bf16[128,640]{1,0:T(8,128)(2,1)S(1)} %concatenate.57) | copy-start | bytes 491524
  107.2 4.6 %copy-start.26 = (bf16[128,640]{1,0:T(8,128)(2,1)}, bf16[128,640]{1,0:T(8,128)(2,1)S(1)}, u32[]{:S(2)}) copy-start(bf16[128,640]{1,0:T(8,128)(2,1)S(1)} %concatenate.58) | copy-start | bytes 491524
  107.2 2.3 %copy-start.31 = (f32[640,320]{0,1:T(8,128)S(1)}, f32[640,320]{0,1:T(8,128)}, u32[]{:S(2)}) copy-start(f32[640,320]{0,1:T(8,128)} %fusion.49) | copy-start | bytes 2457604
  115.8 1.3 copy-start.9
  115.8 1.5 copy-start.11
  115.8 4.7 %copy-start.1 = (bf16[512,1280]{1,0:T(8,128)(2,1)S(1)}, bf16[512,1280]{1,0:T(8,128)(2,1)}, u32[]{:S(2)}) copy-start(bf16[512,1280]{1,0:T(8,128)(2,1)} %copy-done) | copy-start | bytes 3932164
  115.8 82.3 %reduce-scatter.3.cloned.1.call-start = ((), (), s32[]{:S(2)}) async-start(), calls=%async_computation.2 | async-start | bytes 4096000 | tf_op jit(solution)/shard_map/reduce_scatter | solution.py:374
  117.3 3.2 %copy-start.13 = (bf16[128,640]{1,0:T(8,128)(2,1)S(1)}, bf16[128,640]{1,0:T(8,128)(2,1)}, u32[]{:S(2)}) copy-start(bf16[128,640]{1,0:T(8,128)(2,1)} %copy-done.12) | copy-start | bytes 491524
  117.4 3.2 %copy-start.16 = (bf16[128,640]{1,0:T(8,128)(2,1)S(1)}, bf16[128,640]{1,0:T(8,128)(2,1)}, u32[]{:S(2)}) copy-start(bf16[128,640]{1,0:T(8,128)(2,1)} %copy-done.15) | copy-start | bytes 491524
  119.8 1.6 copy-start.25
  119.8 1.6 copy-start.27
  119.8 1.6 copy-start.34
  123.7 1.6 copy-start.32
  127.6 3.6 %copy-start.20 = (bf16[640,320]{0,1:T(8,128)(2,1)}, bf16[640,320]{0,1:T(8,128)(2,1)S(1)}, u32[]{:S(2)}) copy-start(bf16[640,320]{0,1:T(8,128)(2,1)S(1)} %get-tuple-element.21) | copy-start | bytes 1228804
  127.6 1.3 copy-start.30
  135.3 2.3 %copy-start.23 = (bf16[640,320]{0,1:T(8,128)(2,1)S(1)}, bf16[640,320]{0,1:T(8,128)(2,1)}, u32[]{:S(2)}) copy-start(bf16[640,320]{0,1:T(8,128)(2,1)} %copy-done.22) | copy-start | bytes 1228804
  137.6 2.3 %copy-start.21 = (bf16[640,320]{0,1:T(8,128)(2,1)S(1)}, bf16[640,320]{0,1:T(8,128)(2,1)}, u32[]{:S(2)}) copy-start(bf16[640,320]{0,1:T(8,128)(2,1)} %copy-done.20) | copy-start | bytes 1228804
  139.8 2.5 %copy-start.2 = (bf16[512,1280]{1,0:T(8,128)(2,1)S(1)}, bf16[512,1280]{1,0:T(8,128)(2,1)}, u32[]{:S(2)}) copy-start(bf16[512,1280]{1,0:T(8,128)(2,1)} %copy-done) | copy-start | bytes 3932164
  139.8 2.5 %copy-start.14 = (bf16[128,640]{1,0:T(8,128)(2,1)S(1)}, bf16[128,640]{1,0:T(8,128)(2,1)}, u32[]{:S(2)}) copy-start(bf16[128,640]{1,0:T(8,128)(2,1)} %copy-done.12) | copy-start | bytes 491524
  139.9 2.5 %copy-start.17 = (bf16[128,640]{1,0:T(8,128)(2,1)S(1)}, bf16[128,640]{1,0:T(8,128)(2,1)}, u32[]{:S(2)}) copy-start(bf16[128,640]{1,0:T(8,128)(2,1)} %copy-done.15) | copy-start | bytes 491524
  139.9 2.5 %copy-start.36 = (bf16[640,320]{0,1:T(8,128)(2,1)S(1)}, bf16[640,320]{0,1:T(8,128)(2,1)}, u32[]{:S(2)}) copy-start(bf16[640,320]{0,1:T(8,128)(2,1)} %copy-done.35) | copy-start | bytes 1228804
  148.4 45.0 %copy-start.28 = (f32[1280]{0:T(1024)S(1)}, f32[1280]{0:T(1024)}, u32[]{:S(2)}) copy-start(f32[1280]{0:T(1024)} %param.8) | copy-start | bytes 15364
  148.4 46.3 %copy-start.3 = (bf16[128,1280]{1,0:T(8,128)(2,1)S(1)}, bf16[128,1280]{1,0:T(8,128)(2,1)}, u32[]{:S(2)}) copy-start(bf16[128,1280]{1,0:T(8,128)(2,1)} %param.7) | copy-start | bytes 983044
  148.4 48.1 %copy-start.7 = (bf16[128,1280]{1,0:T(8,128)(2,1)S(1)}, bf16[128,1280]{1,0:T(8,128)(2,1)}, u32[]{:S(2)}) copy-start(bf16[128,1280]{1,0:T(8,128)(2,1)} %param.13) | copy-start | bytes 983044
  (7 other events, 7.1 us)
Sparse Core Ops, SparseCore 0:
  116.0 36.8 reduce-scatter.4
  156.0 42.0 reduce-scatter.2
